TPU v7x, 512 devices: a whole 4x8x8 slice. The times are simulated.
512 devices in a mesh: seq: 32 (over z, x), tensor: 16 (over y, core).
Axes of the slice: x: 4, y: 8, z: 8, core: 2. Of those that a mesh axis runs over, the one named last changes fastest.
Arguments:
- queries: bfloat16 [4096, 32, 128], P('seq', 'tensor'), may hold values from -6 to 6
- keys: bfloat16 [2, 4096, 32, 128], P(None, 'seq', 'tensor'), may hold values from -6 to 6
- values: bfloat16 [2, 4096, 32, 128], P(None, 'seq', 'tensor'), may hold values from -24 to 24
- beta: float32 [2, 32, 4096], P(None, 'tensor', 'seq'), may hold values from 0.25 to 2
- decay: float32 [32, 4096], P('tensor', 'seq'), may hold values from -0.75 to 0
- out_gain: float32 [128], replicated, may hold values from 0.1 to 1.9
- residual: bfloat16 [4096, 4096], P('seq', 'tensor'), may hold values from -40 to 40
- ffn_gain: float32 [4096], replicated, may hold values from 0.1 to 1.9
- up_blocks: bfloat16 [64, 16, 128, 128], P('tensor'), may hold values from -0.125 to 0.125
- up_index: int32 [64, 16], P('tensor'), may hold values from 0 to 31, as said below
- down_kept_tiles: bfloat16 [64, 16, 128, 128], P('tensor'), may hold values from -0.09375 to 0.09375
- down_index: int32 [64, 16], P('tensor'), may hold values from 0 to 31, as said below
Outputs:
- layer_out: bfloat16 [4096, 4096], P('seq', 'tensor')
Inputs may be any that keep to these rules, and one draw needn't show every extreme that they name: `up_index`: each row names 16 different tiles. `down_index`: each row names 16 different tiles.
All inputs are finite; a program needn't handle non-finite values.
Results may differ from a plain program's by a relative error of at most 0.014.
Values may be sent and summed in bfloat16 or wider, within the bound.
A program may use at most 64 MiB of HBM per device.

v0:
```python
import jax
import jax.numpy as jnp
from jax import lax
from jax.sharding import PartitionSpec as P

BLOCK_TOK = 64


def entering(value, axis, combine, identity):
    count, index = (lax.axis_size(axis), lax.axis_index(axis))
    everything = jax.tree.map(
        lambda part, kind: lax.all_gather(part.astype(kind), axis),
        value,
        (jnp.bfloat16, jnp.bfloat16),
    )
    start = jax.tree.map(
        lambda part, zero: jnp.broadcast_to(jnp.asarray(zero, part.dtype), part.shape),
        value,
        identity,
    )

    def lap(k, before):
        reached = k < index
        new = combine(
            before, jax.tree.map(lambda part, own: part[k].astype(own.dtype), everything, value)
        )
        return jax.tree.map(lambda a, b: jnp.where(reached, a, b), new, before)

    return lax.fori_loop(0, count, lap, start)


def normed(given):
    wide = given.astype(jnp.float32)
    return wide * lax.rsqrt(jnp.sum(wide * wide, -1, keepdims=True) + 1e-06)


def product(left, right):
    return jnp.einsum("hde,hef->hdf", left, right, precision=lax.Precision.HIGHEST)


def block_terms(queries, keys, values, beta, decay):
    highest = lax.Precision.HIGHEST
    tok_count, heads_dev, width = queries.shape
    span = 2 * BLOCK_TOK
    blocks = tok_count // BLOCK_TOK
    key_unit = normed(keys).transpose(2, 1, 0, 3).reshape(heads_dev, blocks, span, width)
    value_all = (
        values.astype(jnp.float32).transpose(2, 1, 0, 3).reshape(heads_dev, blocks, span, width)
    )
    beta_all = beta.transpose(1, 2, 0).reshape(heads_dev, blocks, span)
    log_gate = jnp.stack([decay, jnp.zeros_like(decay)], -1).reshape(heads_dev, blocks, span)
    query_unit = normed(queries).transpose(1, 0, 2).reshape(heads_dev, blocks, BLOCK_TOK, width)
    running = jnp.cumsum(log_gate, -1)
    rows_at = lax.broadcasted_iota(jnp.int32, (span, span), 0)
    cols_at = lax.broadcasted_iota(jnp.int32, (span, span), 1)
    below = cols_at < rows_at
    key_inner_products = jnp.einsum("hcid,hcmd->hcim", key_unit, key_unit, precision=highest)
    spread = running[..., :, None] - running[..., None, :]
    factor_decay = jnp.exp(jnp.where(below, spread, 0.0))
    lower_part = jnp.where(below, beta_all[..., :, None] * factor_decay * key_inner_products, 0.0)
    system = jnp.eye(span, dtype=jnp.float32) + lower_part
    gamma = jnp.exp(running)
    rhs = beta_all[..., None] * jnp.concatenate([value_all, gamma[..., None] * key_unit], -1)
    solved = jax.scipy.linalg.solve_triangular(system, rhs, lower=True)
    value_new = solved[..., :width]
    weight_rows = solved[..., width:]
    remain = jnp.exp(running[..., -1:] - running)
    key_scaled = remain[..., None] * key_unit
    eye_wide = jnp.eye(width, dtype=jnp.float32)
    block_trans = gamma[..., -1][..., None, None] * eye_wide - jnp.einsum(
        "hcmd,hcme->hcde", key_scaled, weight_rows, precision=highest
    )
    block_write = jnp.einsum("hcmd,hcme->hcde", key_scaled, value_new, precision=highest)
    query_running = running[..., 1::2]
    token_at = lax.broadcasted_iota(jnp.int32, (BLOCK_TOK, span), 0)
    factor_at = lax.broadcasted_iota(jnp.int32, (BLOCK_TOK, span), 1)
    attained_count = factor_at <= 2 * token_at + 1
    query_key = jnp.einsum("hcrd,hcmd->hcrm", query_unit, key_unit, precision=highest)
    query_spread = query_running[..., :, None] - running[..., None, :]
    mixing = jnp.where(
        attained_count, jnp.exp(jnp.where(attained_count, query_spread, 0.0)) * query_key, 0.0
    )
    query_tilde = jnp.exp(query_running)[..., None] * query_unit - jnp.einsum(
        "hcrm,hcme->hcre", mixing, weight_rows, precision=highest
    )
    local_out = jnp.einsum("hcrm,hcme->hcre", mixing, value_new, precision=highest)
    return (block_trans, block_write, query_tilde, local_out)


def incoming_state(dev_trans, dev_write):
    heads_dev, width = (dev_trans.shape[0], dev_trans.shape[1])
    eye_all = jnp.broadcast_to(jnp.eye(width, dtype=jnp.float32), (heads_dev, width, width))
    empty = jnp.zeros((heads_dev, width, width), jnp.float32)

    def linked(earlier, later):
        return (product(later[0], earlier[0]), product(later[0], earlier[1]) + later[1])

    prefix = entering((dev_trans, dev_write), "seq", linked, (eye_all, empty))
    return prefix[1]


def per_device(
    queries,
    keys,
    values,
    beta,
    decay,
    out_gain,
    residual,
    ffn_gain,
    up_blocks,
    up_index,
    down_kept_tiles,
    down_index,
):
    highest = lax.Precision.HIGHEST
    tok_count, heads_dev, width = queries.shape
    block_trans, block_write, query_tilde, local_out = block_terms(
        queries, keys, values, beta, decay
    )
    trans_seq = jnp.moveaxis(block_trans, 1, 0)
    write_seq = jnp.moveaxis(block_write, 1, 0)
    tilde_seq = jnp.moveaxis(query_tilde, 1, 0)
    local_seq = jnp.moveaxis(local_out, 1, 0)
    eye_all = jnp.broadcast_to(jnp.eye(width, dtype=jnp.float32), (heads_dev, width, width))
    empty = jnp.zeros((heads_dev, width, width), jnp.float32)

    def compose(carry, pair):
        prefix, state = carry
        trans_one, write_one = pair
        return (
            (product(trans_one, prefix), product(trans_one, state) + write_one),
            (prefix, state),
        )

    (dev_trans, dev_write), _ = lax.scan(compose, (eye_all, empty), (trans_seq, write_seq))
    arrived = incoming_state(dev_trans, dev_write)

    def emit(state, pieces):
        trans_one, write_one, tilde_one, local_one = pieces
        result = jnp.einsum("hrd,hde->hre", tilde_one, state, precision=highest) + local_one
        return (product(trans_one, state) + write_one, result)

    _, block_out = lax.scan(emit, arrived, (trans_seq, write_seq, tilde_seq, local_seq))
    head_out = jnp.moveaxis(block_out, 0, 1).reshape(heads_dev, tok_count, width).transpose(1, 0, 2)
    normed_out = (
        head_out * lax.rsqrt(jnp.mean(head_out * head_out, -1, keepdims=True) + 1e-05) * out_gain
    )
    hidden_state = (
        residual.astype(jnp.float32) + normed_out.reshape(tok_count, heads_dev * width)
    ).astype(jnp.bfloat16)
    full_rows = lax.all_gather(hidden_state, "tensor", axis=1, tiled=True)
    full_wide = full_rows.astype(jnp.float32)
    ffn_in = (
        full_wide * lax.rsqrt(jnp.mean(full_wide * full_wide, -1, keepdims=True) + 1e-05) * ffn_gain
    ).astype(jnp.bfloat16)
    tile_side = up_blocks.shape[-1]
    tile_count = ffn_in.shape[1] // tile_side
    group_count = up_blocks.shape[0]
    tiles_in = ffn_in.reshape(tok_count, tile_count, tile_side)
    picked = jnp.take(tiles_in, up_index, axis=1)
    pre_act = jnp.einsum("tcjd,cjdh->tch", picked, up_blocks, preferred_element_type=jnp.float32)
    activation = (
        jax.nn.gelu(pre_act).astype(jnp.bfloat16).reshape(tok_count, group_count * tile_side)
    )
    group_ids = jnp.arange(group_count, dtype=jnp.int32)[:, None]
    placed = (
        jnp.zeros((group_count, tile_count, tile_side, tile_side), jnp.bfloat16)
        .at[group_ids, down_index]
        .set(down_kept_tiles)
    )
    dense_down = placed.transpose(0, 2, 1, 3).reshape(
        group_count * tile_side, tile_count * tile_side
    )
    partial_sum = jnp.dot(activation, dense_down, preferred_element_type=jnp.float32)
    ffn_part = lax.psum_scatter(
        partial_sum.astype(jnp.bfloat16), "tensor", scatter_dimension=1, tiled=True
    ).astype(jnp.float32)
    return (hidden_state.astype(jnp.float32) + ffn_part).astype(jnp.bfloat16)


def solution(mesh):
    placed = (
        P("seq", "tensor", None),
        P(None, "seq", "tensor", None),
        P(None, "seq", "tensor", None),
        P(None, "tensor", "seq"),
        P("tensor", "seq"),
        P(),
        P("seq", "tensor"),
        P(),
        P("tensor", None, None, None),
        P("tensor", None),
        P("tensor", None, None, None),
        P("tensor", None),
    )
    return jax.shard_map(
        per_device, mesh=mesh, in_specs=placed, out_specs=P("seq", "tensor"), check_vma=False
    )
```

profile of v0, /device:TPU:25, one launch (start us, length us, event | category | flops | bytes accessed | tf_op | source)
XLA Modules:
  0.0 388.3 jit_solution(9622261280881543677)
XLA Ops:
  6.6 1.0 copy.66
  7.7 0.8 copy.98
  9.8 1.3 fusion.51
  11.1 1.2 fusion.52
  12.6 0.7 fusion.43
  13.3 39.3 %custom-call.4 = f32[2,2,1,128,128]{3,4,2,1,0:T(8,128)S(1)} custom-call(f32[2,2,1,128,128]{4,3,2,1,0:T(8,128)S(1)} %fusion.43), custom_call_target="InvertDiagBlocksLowerTriangular" | custom-call | tf_op jit(solution)/shard_map/jit(_solve_triangular)/vmap(vmap())/triangular_solve | solution.py:64
  53.1 0.7 fusion.48
  55.1 0.9 broadcast_in_dim.71
  56.0 4.3 %while.40 = (s32[]{:T(128)}, f32[2,128,128]{2,1,0:T(8,128)S(1)}, f32[2,128,128]{2,1,0:T(8,128)}, f32[2,2,128,128]{3,2,1,0:T(8,128)S(1)}, f32[2,2,128,128]{3,2,1,0:T(8,128)S(1)}, /*index=5*/s32[]{:T(128)}, s32[]{:T(128)}) while((s32[]{:T(128)}, f32[2,128,128]{2,1,0:T(8,128)S(1)}, f32[2,128,128]{2,1,0:T(8,128)}, ...), condition=%wide.region_3.4_spmd.clone, body=%wide.region_2.0_spmd.clone.sunk | while | flops 100728832 | bytes 1443426 | solution.py:136
  56.0 0.9 copy.146
  56.9 0.9 convolution_add_fusion.7
  58.1 0.9 copy.146
  59.0 0.9 convolution_add_fusion.7
  60.2 1.5 convert_element_type.70
  62.8 1.1 fusion.71
  63.9 1.0 fusion.72
  66.4 79.1 %all-gather.10.cloned.1.call-done = bf16[64,128,128]{2,1,0:T(8,128)(2,1)} async-done(((bf16[2,128,128]{2,1,0:T(8,128)(2,1)}), bf16[64,128,128]{2,1,0:T(8,128)(2,1)}) %all-gather.10.cloned.1.call-update) | async-done | bytes 2097168 | tf_op jit(solution)/shard_map/all_gather | solution.py:12
  145.4 83.8 %all-gather.8.cloned.1.call-done = bf16[64,128,128]{2,1,0:T(8,128)(2,1)} async-done(((bf16[2,128,128]{2,1,0:T(8,128)(2,1)}), bf16[64,128,128]{2,1,0:T(8,128)(2,1)}) %all-gather.8.cloned.1.call-update) | async-done | bytes 2097168 | tf_op jit(solution)/shard_map/all_gather | solution.py:12
  229.2 36.5 %while.41 = (s32[]{:T(128)}, f32[2,128,128]{2,1,0:T(8,128)S(1)}, s32[]{:T(128)}, bf16[32,2,128,128]{3,2,1,0:T(8,128)(2,1)}, bf16[32,2,128,128]{3,2,1,0:T(8,128)(2,1)}, /*index=5*/s32[]{:T(128)}, s32[]{:T(128)}) while((s32[]{:T(128)}, f32[2,128,128]{2,1,0:T(8,128)S(1)}, s32[]{:T(128)}, bf16[32,2,128,128]{3,2,1,0:T(8,128)(2,1)}, ...), condition=%wide.region_5.6_spmd.clone, body=%wide.region_4.5_spmd.clone.sunk | while | flops 50495492 | bytes 789095 | solution.py:29
  229.2 1.1 fusion.126
  230.4 1.1 fusion.126
  231.5 1.1 fusion.126
  232.7 1.1 fusion.126
  233.8 1.1 fusion.126
  234.9 1.1 fusion.126
  236.1 1.1 fusion.126
  237.2 1.1 fusion.126
  238.4 1.1 fusion.126
  239.5 1.1 fusion.126
  240.6 1.1 fusion.126
  241.8 1.1 fusion.126
  242.9 1.1 fusion.126
  244.1 1.1 fusion.126
  245.2 1.1 fusion.126
  246.4 1.1 fusion.126
  247.5 1.1 fusion.126
  248.6 1.1 fusion.126
  249.8 1.1 fusion.126
  250.9 1.1 fusion.126
  252.1 1.1 fusion.126
  253.2 1.1 fusion.126
  254.3 1.1 fusion.126
  255.5 1.1 fusion.126
  256.6 1.1 fusion.126
  257.8 1.1 fusion.126
  258.9 1.1 fusion.126
  260.0 1.1 fusion.126
  261.2 1.1 fusion.126
  262.3 1.1 fusion.126
  263.5 1.1 fusion.126
  264.6 1.1 fusion.126
  265.8 1.1 while.39
  267.2 0.6 fusion.73
  268.3 3.0 broadcast_in_dim.79
  271.3 10.7 %scatter_fusion = bf16[4,32,128,128]{3,2,1,0:T(8,128)(2,1)} fusion(bf16[4,32,128,128]{3,2,1,0:T(8,128)(2,1)} %broadcast_in_dim.79, s32[64]{0:T(128)S(1)} %reshape.118, bf16[64,128,128]{2,1,0:T(8,128)(2,1)} %bitcast.165), kind=kCustom, calls=%fused_computation.1 | custom fusion | bytes 6291968 | tf_op jit(solution)/shard_map/scatter | solution.py:170
  282.0 6.9 %copy.81 = bf16[4,128,32,128]{3,2,1,0:T(8,128)(2,1)} copy(bf16[4,128,32,128]{3,1,2,0:T(8,128)(2,1)} %bitcast.160) | data formatting | bytes 8388608 | tf_op jit(solution)/shard_map/transpose | solution.py:172
  288.8 20.3 %all-gather.6.cloned.1.call-done = bf16[128,4096]{1,0:T(8,128)(2,1)} async-done(((bf16[128,256]{1,0:T(8,128)(2,1)}), bf16[128,4096]{1,0:T(8,128)(2,1)}) %all-gather.6.cloned.1.call-update) | async-done | bytes 1048592 | tf_op jit(solution)/shard_map/all_gather | solution.py:152
  309.2 1.5 fusion.29
  310.7 1.6 copy_bitcast_fusion
  312.3 2.1 gather_fusion
  314.4 2.7 fusion.62
  317.3 2.6 convolution_convert_fusion
  319.8 60.5 %reduce-scatter.2.cloned.1.call-done = bf16[128,256]{1,0:T(8,128)(2,1)} async-done(((bf16[128,4096]{1,0:T(8,128)(2,1)}), bf16[128,256]{1,0:T(8,128)(2,1)}) %reduce-scatter.2.cloned.1.call-update) | async-done | bytes 65552 | tf_op jit(solution)/shard_map/reduce_scatter | solution.py:176
  380.3 1.5 add_convert_fusion
  (113 shorter events, 8.5 us)
Async XLA Ops:
  6.5 307.9 %copy-start = (bf16[4,16,128,128]{3,2,1,0:T(8,128)(2,1)S(1)}, bf16[4,16,128,128]{3,2,1,0:T(8,128)(2,1)}, u32[]{:S(2)}) copy-start(bf16[4,16,128,128]{3,2,1,0:T(8,128)(2,1)} %param.26) | copy-start | bytes 6291460
  6.5 46.1 %copy-start.5 = (bf16[2,128,2,128]{3,2,1,0:T(2,128)(2,1)S(1)}, bf16[2,128,2,128]{3,2,1,0:T(2,128)(2,1)}, u32[]{:S(2)}) copy-start(bf16[2,128,2,128]{3,2,1,0:T(2,128)(2,1)} %param.20) | copy-start | bytes 393220
  6.5 138.9 %all-gather.10.cloned.1.call-start = ((), (), s32[]{:S(2)}) async-start(), calls=%async_computation.4 | async-start | bytes 2162688 | tf_op jit(solution)/shard_map/all_gather | solution.py:12
  6.6 47.9 %copy-start.2 = (f32[128,128]{1,0:T(8,128)}, f32[128,128]{1,0:T(8,128)S(1)}, u32[]{:S(2)}) copy-start(f32[128,128]{1,0:T(8,128)S(1)} %fusion.76) | copy-start | bytes 196612
  61.8 167.4 %all-gather.8.cloned.1.call-start = ((), (), s32[]{:S(2)}) async-start(), calls=%async_computation.3 | async-start | bytes 2162688 | tf_op jit(solution)/shard_map/all_gather | solution.py:12
  62.5 246.6 %all-gather.6.cloned.1.call-start = ((), (), s32[]{:S(2)}) async-start(), calls=%async_computation.1 | async-start | bytes 1114112 | tf_op jit(solution)/shard_map/all_gather | solution.py:152
  66.4 199.3 %copy-start.4 = (f32[2,2,64,128]{3,2,0,1:T(8,128)S(1)}, f32[2,2,64,128]{3,2,0,1:T(8,128)}, u32[]{:S(2)}) copy-start(f32[2,2,64,128]{3,2,0,1:T(8,128)} %custom-call.11) | copy-start | bytes 393220
  265.7 1.3 copy-start.10
  265.7 1.4 copy-start.6
  265.8 2.3 copy-start.9
  265.8 2.4 copy-start.8
  267.8 112.5 %reduce-scatter.2.cloned.1.call-start = ((), (), s32[]{:S(2)}) async-start(), calls=%async_computation.2 | async-start | bytes 1114112 | tf_op jit(solution)/shard_map/reduce_scatter | solution.py:176
  282.0 28.7 %copy-start.7 = (f32[4096]{0:T(1024)S(1)}, f32[4096]{0:T(1024)}, u32[]{:S(2)}) copy-start(f32[4096]{0:T(1024)} %param.25) | copy-start | bytes 49156
  314.4 2.8 copy-start.1
  317.3 63.1 %copy-start.3 = (bf16[128,256]{1,0:T(8,128)(2,1)S(1)}, bf16[128,256]{1,0:T(8,128)(2,1)}, u32[]{:S(2)}) copy-start(bf16[128,256]{1,0:T(8,128)(2,1)} %fusion.73) | copy-start | bytes 196612
Sparse Core Ops, SparseCore 0:
  61.9 83.4 all-gather.9
  148.6 80.5 all-gather.7
  267.9 41.1 all-gather.5
  320.0 60.3 reduce-scatter.1
where the time goes:
time: 390 us; the launch traced here: 388 us
  waiting for transfers between devices  244 us (63%)
  other arithmetic  52.8 us (14%)
  matrix products  47.6 us (12%)
  local copies, waits for them, and re-layouts  29.1 us (7%)
  between operations  13.5 us (3%)
    all_gather x2, waiting for transfers between devices, entering(): lax.all_gather(part.astype(kind), axis)  163 us
    reduce_scatter x1, waiting for transfers between devices, per_device(): lax.psum_scatter(partial_sum.astype(jnp.bfloat16), 'tensor', scatter_dime...  60.5 us
    another operation x1, other arithmetic, block_terms(): solved = jax.scipy.linalg.solve_triangular(system, rhs, lower=True)  39.3 us
    dot_general x38, matrix products, product(): jnp.einsum('hde,hef->hdf', left, right, precision=lax.Precision.HIGHEST)  37.9 us
    all_gather x1, waiting for transfers between devices, per_device(): full_rows = lax.all_gather(hidden_state, 'tensor', axis=1, tiled=True)  20.3 us
    scatter x1, local copies, waits for them, and re-layouts, per_device(): placed = jnp.zeros((group_count, tile_count, tile_side, tile_side), jnp.b...  10.7 us
  transfers between devices with their start and end apart: 4, of which 4 were waited for; matrix products, arithmetic and copies ran while one was open for 6% of the time, Pallas kernels for 0%

commit v1 on v0

v1 whole, which is shorter than its diff:
```python
import functools

import jax
import jax.numpy as jnp
from jax import lax
from jax.experimental import pallas as pl
from jax.experimental.pallas import tpu as pltpu
from jax.sharding import PartitionSpec as P

F32 = jnp.float32
BF16 = jnp.bfloat16
HIGHEST = lax.Precision.HIGHEST
LANES_X = 4
MESH = pl.DeviceIdType.MESH


def dot(a, b, contract=(1, 0), precision=None):
    return lax.dot_general(
        a,
        b,
        (((contract[0],), (contract[1],)), ((), ())),
        precision=precision,
        preferred_element_type=F32,
    )


def split(a):
    high = a.astype(BF16)
    return high, (a - high.astype(F32)).astype(BF16)


def mm3(a, b):
    ah, al = split(a)
    bh, bl = split(b)
    left = jnp.concatenate([ah, al], 1)
    right = jnp.concatenate(
        [jnp.concatenate([bh, bl], 1), jnp.concatenate([bh, jnp.zeros_like(bl)], 1)], 0
    )
    both = dot(left, right)
    n = b.shape[1]
    return both[:, :n] + both[:, n:]


def iota(shape, axis):
    return lax.broadcasted_iota(jnp.int32, shape, axis)


def unit_lower_inverse(lowers):
    n = lowers[0].shape[0]
    rows, cols = iota((n, n), 0), iota((n, n), 1)
    eye = (rows == cols).astype(F32)
    base = (rows >> 3) == (cols >> 3)
    n1 = [jnp.where(base, -low, 0.0) for low in lowers]
    n2 = [mm3(a, a) for a in n1]
    n3 = [mm3(a, b) for a, b in zip(n1, n2)]
    n4 = [mm3(a, a) for a in n2]
    y = [eye + a + b + c for a, b, c in zip(n1, n2, n3)]
    x = [a + mm3(a, b) for a, b in zip(y, n4)]
    shift = 3
    while (1 << shift) < n:
        pick = ((rows >> (shift + 1)) == (cols >> (shift + 1))) & ((rows >> shift) != (cols >> shift))
        links = [jnp.where(pick, low, 0.0) for low in lowers]
        right = [mm3(c, a) for c, a in zip(links, x)]
        x = [a - mm3(a, b) for a, b in zip(x, right)]
        shift += 1
    return x


def local_kernel(
    q_ref, k_ref, v_ref, beta_ref, decay_ref, up_ref, down_ref, tw_ref, qt_ref, lo_ref, inv_ref
):
    tok = q_ref.shape[0] // 2
    span = 2 * tok
    heads = 2
    half = span // 2

    for which, table in enumerate((up_ref, down_ref)):
        for c in range(table.shape[0]):
            for b in range(inv_ref.shape[2]):
                inv_ref[which, c, b] = table.shape[1]
            for j in range(table.shape[1]):
                inv_ref[which, c, table[c, j]] = j

    kv = jnp.concatenate([k_ref[...], v_ref[...]], 1)
    q_all = q_ref[...]
    small = jnp.concatenate(
        [decay_ref[...], beta_ref[0], beta_ref[1], jnp.zeros((2, tok), F32)], 0
    )
    m_at, t_at = iota((span, tok), 0), iota((span, tok), 1)
    upto = (t_at <= (m_at >> 1)).astype(F32)
    first = ((t_at == (m_at >> 1)) & ((m_at & 1) == 0)).astype(F32)
    second = ((t_at == (m_at >> 1)) & ((m_at & 1) == 1)).astype(F32)
    upto_tok = (iota((tok, tok), 1) <= iota((tok, tok), 0)).astype(F32)
    run_col = dot(upto, small, (1, 1), HIGHEST)
    run_row = dot(small, upto, (1, 1), HIGHEST)
    tok_col = dot(upto_tok, small, (1, 1), HIGHEST)
    one_col, two_col = dot(first, small, (1, 1), HIGHEST), dot(second, small, (1, 1), HIGHEST)
    one_row, two_row = dot(small, first, (1, 1), HIGHEST), dot(small, second, (1, 1), HIGHEST)

    rows, cols = iota((span, span), 0), iota((span, span), 1)
    below = cols < rows
    same = rows == cols
    reach = iota((tok, span), 1) <= 2 * iota((tok, span), 0) + 1
    eye = (iota((tok, tok), 0) == iota((tok, tok), 1)).astype(F32)
    row_of = iota((span, 4 * tok), 0)
    place = (row_of & 1) * span + (row_of >> 1) * 2
    column = iota((span, 4 * tok), 1)
    q_place = iota((tok, span), 0) * 2
    q_column = iota((tok, span), 1)

    ks, vs, qs, gammas, lowers, keep = [], [], [], [], [], []
    for h in range(heads):
        pick = (column == place + h).astype(BF16)
        both = dot(pick, kv).astype(BF16)
        k, v = both[:, :128], both[:, 128:]
        q = dot((q_column == q_place + h).astype(BF16), q_all)
        gram = dot(k, k, (1, 1))
        diag = jnp.where(same, gram, 0.0)
        rk_col = lax.rsqrt(jnp.sum(diag, 1, keepdims=True) + 1e-06)
        rk_row = lax.rsqrt(jnp.sum(diag, 0, keepdims=True) + 1e-06)
        run_c, run_r = run_col[:, h : h + 1], run_row[h : h + 1, :]
        beta_c = one_col[:, 2 + h : 3 + h] + two_col[:, 4 + h : 5 + h]
        beta_r = one_row[2 + h : 3 + h, :] + two_row[4 + h : 5 + h, :]
        fade = jnp.exp(jnp.where(below, run_c - run_r, 0.0))
        low = jnp.where(below, (beta_c * rk_col) * fade * gram * rk_row, 0.0)
        keep.append((k, v, q, rk_col, rk_row, run_c, run_r, beta_r, low))
        lowers += [low[:half, :half], low[half:, half:]]

    inverses = unit_lower_inverse(lowers)
    mids = [mm3(keep[h][8][half:, :half], inverses[2 * h]) for h in range(heads)]
    crosses = [mm3(inverses[2 * h + 1], mids[h]) for h in range(heads)]
    for h in range(heads):
        k, v, q, rk_col, rk_row, run_c, run_r, beta_r, low = keep[h]
        a = jnp.concatenate(
            [
                jnp.concatenate([inverses[2 * h], jnp.zeros((half, half), F32)], 1),
                jnp.concatenate([-crosses[h], inverses[2 * h + 1]], 1),
            ],
            0,
        )
        a_val = a * beta_r
        a_key = a_val * (jnp.exp(run_r) * rk_row)
        ah, al = split(a_val)
        u = dot(ah, v) + dot(al, v)
        ah, al = split(a_key)
        w = dot(ah, k) + dot(al, k)
        last = run_c[span - 1 : span, :]
        remain = jnp.exp(last - run_c) * rk_col
        uh, ul = split(u * remain)
        write_t = dot(uh, k, (0, 0)) + dot(ul, k, (0, 0))
        wh, wl = split(w * remain)
        trans = jnp.exp(last) * eye - dot(k, wh, (0, 0)) - dot(k, wl, (0, 0))
        tw_ref[h, 0:64, :] = write_t[:64].astype(BF16)
        tw_ref[h, 64:192, :] = trans.astype(BF16)
        tw_ref[h, 192:256, :] = write_t[64:].astype(BF16)
        tok_run = tok_col[:, h : h + 1]
        rq = lax.rsqrt(jnp.sum(q * q, 1, keepdims=True) + 1e-06)
        qk = dot(q.astype(BF16), k, (1, 1))
        mixing = jnp.where(
            reach, jnp.exp(jnp.where(reach, tok_run - run_r, 0.0)) * qk * rq * rk_row, 0.0
        )
        mh, ml = split(mixing)
        bh, bl = split(jnp.concatenate([w, u], 1))
        mixed = dot(mh, bh) + dot(ml, bh) + dot(mh, bl)
        qt_ref[h] = (jnp.exp(tok_run) * rq) * q - mixed[:, :128]
        lo_ref[h] = mixed[:, 128:]


def chain_step(state, trans, write):
    n = state.shape[0]
    high, low = split(state)
    both = dot(jnp.concatenate([high, low], 0), trans, (1, 1))
    return both[:n] + both[n:] + write.astype(F32)


def main_kernel(
    nz,
    ny,
    inv_ref,
    tw_ref,
    qt_ref,
    lo_ref,
    res_ref,
    og_ref,
    fg_ref,
    up_hbm,
    down_hbm,
    out_ref,
    up_v,
    down_v,
    rx,
    zmsg,
    rz,
    chain,
    pmsg,
    rp,
    xg,
    acc,
    act,
    pair_out,
    pair_in,
    psum,
    rs,
    wsem,
    a_send,
    a_recv,
    b_send,
    b_recv,
    c_send,
    c_recv,
    z_send,
    z_recv,
    p_send,
    p_recv,
    g_send,
    g_recv,
    f_send,
    s_send,
    s_recv,
    r_send,
    r_recv,
):
    seq, ten = lax.axis_index("seq"), lax.axis_index("tensor")
    z, x = seq // LANES_X, lax.rem(seq, LANES_X)
    y, core = ten // 2, lax.rem(ten, 2)
    partner = y * 2 + 1 - core
    head, part = x // 2, lax.rem(x, 2)
    groups = up_hbm.shape[0]
    kept = up_hbm.shape[1]

    def at_x(o):
        return lax.rem(x + o, LANES_X)

    def at_y(o):
        return lax.rem(y + o, ny)

    barrier = pltpu.get_barrier_semaphore()
    peers = [(z * LANES_X + at_x(o), ten) for o in range(1, LANES_X)]
    peers += [(lax.rem(z + o, nz) * LANES_X + x, ten) for o in range(1, nz)]
    peers += [(seq, at_y(o) * 2 + core) for o in range(1, ny)]
    peers += [(seq, partner)]
    for peer in peers:
        pl.semaphore_signal(barrier, inc=1, device_id=peer, device_id_type=MESH)

    load_up = pltpu.make_async_copy(up_hbm, up_v.at[:, pl.ds(0, kept)], wsem.at[0])
    load_down = pltpu.make_async_copy(down_hbm, down_v.at[:, pl.ds(0, kept)], wsem.at[1])
    load_up.start()
    load_down.start()
    rx[x] = tw_ref[...]
    for c in range(groups):
        up_v[c, kept] = jnp.zeros(up_v.shape[2:], BF16)
        down_v[c, kept] = jnp.zeros(up_v.shape[2:], BF16)
    chain[...] = jnp.zeros_like(chain)
    pl.semaphore_wait(barrier, len(peers))

    def remote(src, dst, send, recv, peer):
        return pltpu.make_async_remote_copy(
            src_ref=src,
            dst_ref=dst,
            send_sem=send,
            recv_sem=recv,
            device_id=peer,
            device_id_type=MESH,
        )

    def a_copy(o):
        there = at_x(o)
        h2, p2 = there // 2, lax.rem(there, 2)
        rows = pl.ds(pl.multiple_of(p2 * 64, 64), 192)
        return remote(
            tw_ref.at[h2, rows],
            rx.at[x, h2, rows],
            a_send.at[o],
            a_recv.at[x],
            (z * LANES_X + there, ten),
        )

    def b_copies(o):
        there = at_x(o)
        h2, p2 = there // 2, lax.rem(there, 2)
        rows = pl.ds(pl.multiple_of((1 - p2) * 192, 64), 64)
        peer = (z * LANES_X + there, ten)
        return (
            remote(
                tw_ref.at[h2, rows], rx.at[x, h2, rows], b_send.at[o], b_recv.at[x], peer
            ),
            remote(
                tw_ref.at[1 - h2], rx.at[x, 1 - h2], c_send.at[o], c_recv.at[x], peer
            ),
        )

    for o in (2, 1, 3):
        a_copy(o).start()
    for o in range(1, LANES_X):

        @pl.when(x + o < LANES_X)
        def _():
            for one in b_copies(o):
                one.start()

    my_rows = pl.ds(pl.multiple_of(part * 64, 64), 192)
    for o in (1, 3, 2):
        source = at_x(o)
        remote(
            rx.at[source, head, my_rows],
            rx.at[source, head, my_rows],
            a_send.at[o],
            a_recv.at[source],
            (seq, ten),
        ).wait_recv()

    w_rows = pl.ds(pl.multiple_of(part * 192, 64), 64)
    ts = [rx[i, head, pl.ds(64, 128)] for i in range(LANES_X)]
    ws = [rx[i, head, w_rows] for i in range(LANES_X)]
    t10, t32 = dot(ts[1], ts[0]), dot(ts[3], ts[2])
    w10 = dot(ws[0], ts[1], (1, 1)) + ws[1].astype(F32)
    w32 = dot(ws[2], ts[3], (1, 1)) + ws[3].astype(F32)
    zmsg[64:192] = mm3(t32, t10).astype(BF16)
    th, tl = split(t32)
    wh, wl = split(w10)
    mixed = dot(jnp.concatenate([wh, wl], 0), th, (1, 1))
    w_all = mixed[:64] + mixed[64:] + dot(wh, tl, (1, 1)) + w32
    zmsg[0:64] = w_all.astype(BF16)

    def z_copy(o):
        return remote(
            zmsg,
            rz.at[z],
            z_send.at[o],
            z_recv.at[z],
            ((z + o) * LANES_X + x, ten),
        )

    for o in range(1, nz):

        @pl.when(z + o < nz)
        def _():
            z_copy(o).start()

    for i in range(nz - 1):

        @pl.when(i < z)
        def _():
            remote(
                rz.at[i], rz.at[i], z_send.at[0], z_recv.at[i], (seq, ten)
            ).wait_recv()
            if i == 0:
                chain[...] = rz[0, 0:64].astype(F32)
            else:
                chain[...] = chain_step(chain[...], rz[i, 64:192], rz[i, 0:64])

    entering = chain[...].astype(BF16)
    pmsg[...] = entering
    p_rows = pl.ds(pl.multiple_of(part * 64, 64), 64)
    rp[head, p_rows] = entering

    def p_copy(o):
        return remote(
            pmsg,
            rp.at[head, p_rows],
            p_send.at[o],
            p_recv.at[x],
            (z * LANES_X + at_x(o), ten),
        )

    for o in (2, 1, 3):
        p_copy(o).start()
    for i in range(LANES_X - 1):

        @pl.when(i < x)
        def _():
            other = pl.ds(pl.multiple_of((1 - part) * 192, 64), 64)
            remote(
                rx.at[i, head, other],
                rx.at[i, head, other],
                b_send.at[0],
                b_recv.at[i],
                (seq, ten),
            ).wait_recv()
            remote(
                rx.at[i, 1 - head], rx.at[i, 1 - head], c_send.at[0], c_recv.at[i], (seq, ten)
            ).wait_recv()

    for o in (1, 3, 2):
        source = at_x(o)
        rows = pl.ds(pl.multiple_of(lax.rem(source, 2) * 64, 64), 64)
        remote(
            rp.at[source // 2, rows],
            rp.at[source // 2, rows],
            p_send.at[o],
            p_recv.at[source],
            (seq, ten),
        ).wait_recv()

    state = [rp[h].astype(F32) for h in range(2)]
    for i in range(LANES_X - 1):
        for h in range(2):
            write = jnp.concatenate([rx[i, h, 0:64], rx[i, h, 192:256]], 0)
            moved = chain_step(state[h], rx[i, h, 64:192], write)
            state[h] = jnp.where(i < x, moved, state[h])

    gain = og_ref[...]
    pieces = []
    for h in range(2):
        qh, ql = split(qt_ref[h])
        sh, sl = split(state[h])
        head_out = dot(qh, sh, (1, 1)) + dot(ql, sh, (1, 1)) + dot(qh, sl, (1, 1)) + lo_ref[h]
        power = jnp.mean(head_out * head_out, -1, keepdims=True)
        normed = head_out * lax.rsqrt(power + 1e-05) * gain
        pieces.append(res_ref[:, 128 * h : 128 * h + 128].astype(F32) + normed)
    xg[ten] = jnp.concatenate(pieces, 1).astype(BF16)

    def g_copy(o):
        return remote(
            xg.at[ten],
            xg.at[ten],
            g_send.at[o],
            g_recv.at[ten],
            (seq, partner if o == 0 else at_y(o) * 2 + core),
        )

    order = sorted(range(1, ny), key=lambda o: -min(o, ny - o))
    for o in order:
        g_copy(o).start()
    g_copy(0).start()

    def f_copy(o):
        slot = at_y(o) * 2 + core
        return remote(
            xg.at[slot], xg.at[slot], f_send.at[o], g_recv.at[slot], (seq, partner)
        )

    def arrived(slot):
        remote(
            xg.at[slot], xg.at[slot], g_send.at[0], g_recv.at[slot], (seq, ten)
        ).wait_recv()

    load_up.wait()
    load_down.wait()

    def absorb(slot, first, power):
        wide = xg[slot].astype(F32)
        power = power + jnp.sum(wide * wide, -1, keepdims=True)
        scaled = (wide * fg_ref[slot]).astype(BF16)
        weights = jnp.concatenate(
            [
                jnp.concatenate(
                    [up_v[c, inv_ref[0, c, 2 * slot + b]] for c in range(groups)], 1
                )
                for b in range(2)
            ],
            0,
        )
        term = dot(scaled, weights)
        if first:
            acc[...] = term
        else:
            acc[...] += term
        return power

    power = absorb(ten, True, jnp.zeros((xg.shape[1], 1), F32))
    arrived(partner)
    power = absorb(partner, False, power)
    late = None
    for o in sorted(range(1, ny), key=lambda o: (min(o, ny - o), o)):
        slot = at_y(o) * 2 + core
        arrived(slot)
        f_copy(o).start()
        power = absorb(slot, False, power)
        if late is not None:
            arrived(late)
            power = absorb(late, False, power)
        late = at_y(o) * 2 + 1 - core
    if late is not None:
        arrived(late)
        power = absorb(late, False, power)

    width = 256 * xg.shape[0]
    scale = lax.rsqrt(power / width + 1e-05)
    act[...] = jax.nn.gelu(acc[...] * scale).astype(BF16)

    def share(slot):
        weights = jnp.concatenate(
            [
                jnp.concatenate(
                    [down_v[c, inv_ref[1, c, 2 * slot + b]] for b in range(2)], 1
                )
                for c in range(groups)
            ],
            0,
        )
        return dot(act[...], weights).astype(BF16)

    def s_copy(o):
        return remote(
            pair_out.at[o], pair_in.at[o], s_send.at[o], s_recv.at[o], (seq, partner)
        )

    def r_copy(o):
        return remote(
            psum.at[o],
            rs.at[y],
            r_send.at[o],
            r_recv.at[y],
            (seq, at_y(o) * 2 + core),
        )

    for o in order + [0]:
        pair_out[o] = share(at_y(o) * 2 + 1 - core)
        s_copy(o).start()
    total = None
    for o in order + [0]:
        mine = share(at_y(o) * 2 + core).astype(F32)
        s_copy(o).wait_recv()
        summed = mine + pair_in[o].astype(F32)
        if o == 0:
            total = summed
        else:
            psum[o] = summed.astype(BF16)
            r_copy(o).start()
    total = total + xg[ten].astype(F32)
    for o in sorted(range(1, ny), key=lambda o: (min(o, ny - o), o)):
        source = at_y(o)
        remote(
            rs.at[source], rs.at[source], r_send.at[0], r_recv.at[source], (seq, ten)
        ).wait_recv()
        total = total + rs[source].astype(F32)
    out_ref[...] = total.astype(BF16)

    for o in range(1, LANES_X):
        a_copy(o).wait_send()
        p_copy(o).wait_send()

        @pl.when(x + o < LANES_X)
        def _():
            for one in b_copies(o):
                one.wait_send()

    for o in range(1, nz):

        @pl.when(z + o < nz)
        def _():
            z_copy(o).wait_send()

    g_copy(0).wait_send()
    s_copy(0).wait_send()
    for o in range(1, ny):
        g_copy(o).wait_send()
        f_copy(o).wait_send()
        s_copy(o).wait_send()
        r_copy(o).wait_send()


def solution(mesh):
    nseq, nten = mesh.shape["seq"], mesh.shape["tensor"]
    nz, ny = nseq // LANES_X, nten // 2
    vmem = pl.BlockSpec(memory_space=pltpu.VMEM)
    smem = pl.BlockSpec(memory_space=pltpu.SMEM)
    anywhere = pl.BlockSpec(memory_space=pl.ANY)
    dma = pltpu.SemaphoreType.DMA

    def per_device(
        queries,
        keys,
        values,
        beta,
        decay,
        out_gain,
        residual,
        ffn_gain,
        up_blocks,
        up_index,
        down_kept_tiles,
        down_index,
    ):
        tok = queries.shape[0]
        groups, kept = up_index.shape
        tiles = 2 * nten
        tw, qt, lo, inv = pl.pallas_call(
            local_kernel,
            out_shape=(
                jax.ShapeDtypeStruct((2, 256, 128), BF16),
                jax.ShapeDtypeStruct((2, tok, 128), F32),
                jax.ShapeDtypeStruct((2, tok, 128), F32),
                jax.ShapeDtypeStruct((2, groups, tiles), jnp.int32),
            ),
            in_specs=[vmem] * 5 + [smem] * 2,
            out_specs=(vmem, vmem, vmem, smem),
            name="local_terms",
        )(
            queries.reshape(2 * tok, 128),
            keys.reshape(4 * tok, 128),
            values.reshape(4 * tok, 128),
            beta,
            decay,
            up_index,
            down_index,
        )
        return pl.pallas_call(
            functools.partial(main_kernel, nz, ny),
            out_shape=jax.ShapeDtypeStruct((tok, 256), BF16),
            in_specs=[smem] + [vmem] * 6 + [anywhere] * 2,
            out_specs=vmem,
            scratch_shapes=[
                pltpu.VMEM((groups, kept + 1, 128, 128), BF16),
                pltpu.VMEM((groups, kept + 1, 128, 128), BF16),
                pltpu.VMEM((LANES_X, 2, 256, 128), BF16),
                pltpu.VMEM((192, 128), BF16),
                pltpu.VMEM((nz, 192, 128), BF16),
                pltpu.VMEM((64, 128), F32),
                pltpu.VMEM((64, 128), BF16),
                pltpu.VMEM((2, 128, 128), BF16),
                pltpu.VMEM((nten, tok, 256), BF16),
                pltpu.VMEM((tok, groups * 128), F32),
                pltpu.VMEM((tok, groups * 128), BF16),
                pltpu.VMEM((ny, tok, 256), BF16),
                pltpu.VMEM((ny, tok, 256), BF16),
                pltpu.VMEM((ny, tok, 256), BF16),
                pltpu.VMEM((ny, tok, 256), BF16),
                dma((2,)),
                dma((LANES_X,)),
                dma((LANES_X,)),
                dma((LANES_X,)),
                dma((LANES_X,)),
                dma((LANES_X,)),
                dma((LANES_X,)),
                dma((nz,)),
                dma((nz,)),
                dma((LANES_X,)),
                dma((LANES_X,)),
                dma((ny,)),
                dma((nten,)),
                dma((ny,)),
                dma((ny,)),
                dma((ny,)),
                dma((ny,)),
                dma((ny,)),
            ],
            compiler_params=pltpu.CompilerParams(collective_id=0, has_side_effects=True),
            name="scan_and_ffn",
        )(
            inv,
            tw,
            qt,
            lo,
            residual,
            out_gain.reshape(1, 128),
            ffn_gain.reshape(nten, 1, 256),
            up_blocks,
            down_kept_tiles,
        )

    placed = (
        P("seq", "tensor", None),
        P(None, "seq", "tensor", None),
        P(None, "seq", "tensor", None),
        P(None, "tensor", "seq"),
        P("tensor", "seq"),
        P(),
        P("seq", "tensor"),
        P(),
        P("tensor", None, None, None),
        P("tensor", None),
        P("tensor", None, None, None),
        P("tensor", None),
    )
    return jax.shard_map(
        per_device, mesh=mesh, in_specs=placed, out_specs=P("seq", "tensor"), check_vma=False
    )
```

time: 390 us -> 69.9 us (0.18)
  the two profiles are of different devices: /device:TPU:25 before, /device:TPU:392 now
where the time goes in v1:
time: 69.9 us; the launch traced here: 69.7 us
  Pallas kernels  68.2 us (98%)
  local copies, waits for them, and re-layouts  1.47 us (2%)
    pallas_call x1, Pallas kernels, per_device(): pl.pallas_call(functools.partial(main_kernel, nz, ny), out_shape=jax.Shap...  61.2 us
    pallas_call x1, Pallas kernels, per_device(): pl.pallas_call(local_kernel, out_shape=(jax.ShapeDtypeStruct((2, 256, 128...  6.97 us
    unnamed x1, local copies, waits for them, and re-layouts  1.47 us

profile of v1, /device:TPU:392, one launch (start us, length us, event | category | flops | bytes accessed | tf_op | source)
XLA Modules:
  0.0 69.7 jit_solution(13043556233034063515)
XLA Ops:
  0.0 7.0 %local_terms.1 = (bf16[2,256,128]{2,1,0:T(8,128)(2,1)}, f32[2,128,128]{2,1,0:T(8,128)}, f32[2,128,128]{2,1,0:T(8,128)}, s32[2,4,32]{2,1,0:T(4,128)}) custom-call(bf16[256,128]{1,0:T(8,128)(2,1)} %bitcast.7, bf16[512,128]{1,0:T(8,128)(2,1)} %bitcast.5, bf16[512,128]{1,0:T(8,128)(2,1)} %bitcast.6, f32[2,2,128]{2,1,0:T(2,128)} %beta_ref.1, f32[2,128]{1,0:T(2,128)} %decay_ref.1, ...), custom_call_target="tpu_custom_call" | custom-call | tf_op jit(solution)/shard_map/local_terms/pallas_call | solution.py:579
  7.0 61.2 %scan_and_ffn.1 = bf16[128,256]{1,0:T(8,128)(2,1)} custom-call(s32[2,4,32]{2,1,0:T(4,128)} %get-tuple-element.9.inv_ref, bf16[2,256,128]{2,1,0:T(8,128)(2,1)} %get-tuple-element.10.tw_ref, f32[2,128,128]{2,1,0:T(8,128)} %get-tuple-element.11.qt_ref, f32[2,128,128]{2,1,0:T(8,128)} %get-tuple-element.12.lo_ref, bf16[128,256]{1,0:T(8,128)(2,1)} %res_ref.1, ...), custom_call_target="tpu_custom_call" | custom-call | tf_op jit(solution)/shard_map/scan_and_ffn/pallas_call | solution.py:599
  68.2 1.5 %copy.14 = bf16[128,256]{1,0:T(8,128)(2,1)} copy(bf16[128,256]{1,0:T(8,128)(2,1)} %scan_and_ffn.1) | data formatting | bytes 131072

commit v2 on v1

--- a/solution.py
+++ b/solution.py
@@ -215,6 +215,8 @@
     g_send,
     g_recv,
     f_send,
+    f_recv,
+    o_sem,
     s_send,
     s_recv,
     r_send,
@@ -291,13 +293,6 @@
 
     for o in (2, 1, 3):
         a_copy(o).start()
-    for o in range(1, LANES_X):
-
-        @pl.when(x + o < LANES_X)
-        def _():
-            for one in b_copies(o):
-                one.start()
-
     my_rows = pl.ds(pl.multiple_of(part * 64, 64), 192)
     for o in (1, 3, 2):
         source = at_x(o)
@@ -336,6 +331,13 @@
         @pl.when(z + o < nz)
         def _():
             z_copy(o).start()
+
+    for o in range(1, LANES_X):
+
+        @pl.when(x + o < LANES_X)
+        def _():
+            for one in b_copies(o):
+                one.start()
 
     for i in range(nz - 1):
 
@@ -410,30 +412,47 @@
         pieces.append(res_ref[:, 128 * h : 128 * h + 128].astype(F32) + normed)
     xg[ten] = jnp.concatenate(pieces, 1).astype(BF16)
 
-    def g_copy(o):
-        return remote(
-            xg.at[ten],
-            xg.at[ten],
-            g_send.at[o],
-            g_recv.at[ten],
-            (seq, partner if o == 0 else at_y(o) * 2 + core),
-        )
-
-    order = sorted(range(1, ny), key=lambda o: -min(o, ny - o))
-    for o in order:
-        g_copy(o).start()
-    g_copy(0).start()
-
-    def f_copy(o):
-        slot = at_y(o) * 2 + core
-        return remote(
-            xg.at[slot], xg.at[slot], f_send.at[o], g_recv.at[slot], (seq, partner)
-        )
-
-    def arrived(slot):
-        remote(
-            xg.at[slot], xg.at[slot], g_send.at[0], g_recv.at[slot], (seq, ten)
-        ).wait_recv()
+    reach = ny // 2
+    ways = (1, -1)
+    halves = [pl.ds(0, xg.shape[1] // 2), pl.ds(xg.shape[1] // 2, xg.shape[1] // 2)]
+
+    def sent(i, d, part_at):
+        return d < reach or part_at == i
+
+    messages = [
+        (i, d, p)
+        for d in range(1, reach + 1)
+        for p in range(2)
+        for i in range(2)
+        if sent(i, d, p)
+    ]
+
+    def neighbour(i):
+        return (seq, at_y(ways[i] + ny) * 2 + core)
+
+    def ring(i, d, p):
+        block = xg.at[at_y(ny - ways[i] * (d - 1)) * 2 + core, halves[p]]
+        return remote(block, block, g_send.at[i, d, p], g_recv.at[i, d, p], neighbour(i))
+
+    def got(i, d, p):
+        block = xg.at[at_y(ny - ways[i] * d) * 2 + core, halves[p]]
+        remote(block, block, g_send.at[i, d, p], g_recv.at[i, d, p], (seq, ten)).wait_recv()
+
+    def pass_on(i, d, p):
+        block = xg.at[at_y(ny - ways[i] * d) * 2 + core, halves[p]]
+        return remote(block, block, f_send.at[i, d, p], f_recv.at[i, d, p], (seq, partner))
+
+    def passed(i, d, p):
+        block = xg.at[at_y(ny - ways[i] * d) * 2 + 1 - core, halves[p]]
+        remote(block, block, f_send.at[i, d, p], f_recv.at[i, d, p], (seq, ten)).wait_recv()
+
+    def own_copy():
+        return remote(xg.at[ten], xg.at[ten], o_sem.at[0], o_sem.at[1], (seq, partner))
+
+    for i, d, p in messages:
+        if d == 1:
+            ring(i, d, p).start()
+    own_copy().start()
 
     load_up.wait()
     load_down.wait()
@@ -458,22 +477,32 @@
             acc[...] += term
         return power
 
+    def blocks(d):
+        return [at_y(d)] if d == reach else [at_y(ny - d), at_y(d)]
+
     power = absorb(ten, True, jnp.zeros((xg.shape[1], 1), F32))
-    arrived(partner)
+    remote(xg.at[partner], xg.at[partner], o_sem.at[0], o_sem.at[1], (seq, ten)).wait_recv()
     power = absorb(partner, False, power)
-    late = None
-    for o in sorted(range(1, ny), key=lambda o: (min(o, ny - o), o)):
-        slot = at_y(o) * 2 + core
-        arrived(slot)
-        f_copy(o).start()
-        power = absorb(slot, False, power)
-        if late is not None:
-            arrived(late)
-            power = absorb(late, False, power)
-        late = at_y(o) * 2 + 1 - core
-    if late is not None:
-        arrived(late)
-        power = absorb(late, False, power)
+    for d in range(1, reach + 1):
+        for i, e, p in messages:
+            if e == d:
+                got(i, d, p)
+                if d < reach and sent(i, d + 1, p):
+                    ring(i, d + 1, p).start()
+                pass_on(i, d, p).start()
+        if d > 1:
+            for i, e, p in messages:
+                if e == d - 1:
+                    passed(i, e, p)
+            for where in blocks(d - 1):
+                power = absorb(where * 2 + 1 - core, False, power)
+        for where in blocks(d):
+            power = absorb(where * 2 + core, False, power)
+    for i, e, p in messages:
+        if e == reach:
+            passed(i, e, p)
+    for where in blocks(reach):
+        power = absorb(where * 2 + 1 - core, False, power)
 
     width = 256 * xg.shape[0]
     scale = lax.rsqrt(power / width + 1e-05)
@@ -491,41 +520,70 @@
         )
         return dot(act[...], weights).astype(BF16)
 
-    def s_copy(o):
+    def s_copy(off):
+        k = off + reach - 1
         return remote(
-            pair_out.at[o], pair_in.at[o], s_send.at[o], s_recv.at[o], (seq, partner)
-        )
-
-    def r_copy(o):
+            pair_out.at[k], pair_in.at[k], s_send.at[k], s_recv.at[k], (seq, partner)
+        )
+
+    def offer(off):
+        pair_out[off + reach - 1] = share(at_y(ny + off) * 2 + 1 - core)
+        s_copy(off).start()
+
+    def pair_sum(off):
+        mine = share(at_y(ny + off) * 2 + core).astype(F32)
+        s_copy(off).wait_recv()
+        return mine + pair_in[off + reach - 1].astype(F32)
+
+    def m_copy(i, d, p):
         return remote(
-            psum.at[o],
-            rs.at[y],
-            r_send.at[o],
-            r_recv.at[y],
-            (seq, at_y(o) * 2 + core),
-        )
-
-    for o in order + [0]:
-        pair_out[o] = share(at_y(o) * 2 + 1 - core)
-        s_copy(o).start()
-    total = None
-    for o in order + [0]:
-        mine = share(at_y(o) * 2 + core).astype(F32)
-        s_copy(o).wait_recv()
-        summed = mine + pair_in[o].astype(F32)
-        if o == 0:
-            total = summed
-        else:
-            psum[o] = summed.astype(BF16)
-            r_copy(o).start()
-    total = total + xg[ten].astype(F32)
-    for o in sorted(range(1, ny), key=lambda o: (min(o, ny - o), o)):
-        source = at_y(o)
-        remote(
-            rs.at[source], rs.at[source], r_send.at[0], r_recv.at[source], (seq, ten)
-        ).wait_recv()
-        total = total + rs[source].astype(F32)
-    out_ref[...] = total.astype(BF16)
+            psum.at[i, d, halves[p]],
+            rs.at[i, d, halves[p]],
+            r_send.at[i, d, p],
+            r_recv.at[i, d, p],
+            neighbour(i),
+        )
+
+    def m_got(i, d, p):
+        block = rs.at[i, d, halves[p]]
+        remote(block, block, r_send.at[i, d, p], r_recv.at[i, d, p], (seq, ten)).wait_recv()
+        return rs[i, d, halves[p]].astype(F32)
+
+    rows_dev = xg.shape[1] // 2
+
+    def rows_of(value, p):
+        return value[p * rows_dev : (p + 1) * rows_dev]
+
+    def offer_level(d):
+        for off in (d, -d) if d else (0,):
+            offer(off)
+
+    offer(reach)
+    offer_level(reach - 1)
+    far = pair_sum(reach)
+    for i in range(2):
+        psum[i, reach, halves[i]] = rows_of(far, i).astype(BF16)
+        m_copy(i, reach, i).start()
+    for d in range(reach - 1, 0, -1):
+        offer_level(d - 1)
+        sums = [pair_sum(d), pair_sum(-d)]
+        for fresh in (True, False):
+            for p in range(2):
+                for i in range(2):
+                    if sent(i, d + 1, p) == fresh:
+                        continue
+                    value = rows_of(sums[i], p)
+                    if not fresh:
+                        value = value + m_got(i, d + 1, p)
+                    psum[i, d, halves[p]] = value.astype(BF16)
+                    m_copy(i, d, p).start()
+    total = pair_sum(0) + xg[ten].astype(F32)
+    for p in range(2):
+        value = rows_of(total, p)
+        for i in range(2):
+            if sent(i, 1, p):
+                value = value + m_got(i, 1, p)
+        out_ref[halves[p], :] = value.astype(BF16)
 
     for o in range(1, LANES_X):
         a_copy(o).wait_send()
@@ -542,13 +600,13 @@
         def _():
             z_copy(o).wait_send()
 
-    g_copy(0).wait_send()
-    s_copy(0).wait_send()
-    for o in range(1, ny):
-        g_copy(o).wait_send()
-        f_copy(o).wait_send()
-        s_copy(o).wait_send()
-        r_copy(o).wait_send()
+    own_copy().wait_send()
+    for off in range(1 - reach, reach + 1):
+        s_copy(off).wait_send()
+    for i, d, p in messages:
+        ring(i, d, p).wait_send()
+        pass_on(i, d, p).wait_send()
+        m_copy(i, d, p).wait_send()
 
 
 def solution(mesh):
@@ -615,8 +673,8 @@
                 pltpu.VMEM((tok, groups * 128), BF16),
                 pltpu.VMEM((ny, tok, 256), BF16),
                 pltpu.VMEM((ny, tok, 256), BF16),
-                pltpu.VMEM((ny, tok, 256), BF16),
-                pltpu.VMEM((ny, tok, 256), BF16),
+                pltpu.VMEM((2, ny // 2 + 1, tok, 256), BF16),
+                pltpu.VMEM((2, ny // 2 + 1, tok, 256), BF16),
                 dma((2,)),
                 dma((LANES_X,)),
                 dma((LANES_X,)),
@@ -628,13 +686,15 @@
                 dma((nz,)),
                 dma((LANES_X,)),
                 dma((LANES_X,)),
-                dma((ny,)),
-                dma((nten,)),
+                dma((2, ny // 2 + 1, 2)),
+                dma((2, ny // 2 + 1, 2)),
+                dma((2, ny // 2 + 1, 2)),
+                dma((2, ny // 2 + 1, 2)),
+                dma((2,)),
                 dma((ny,)),
                 dma((ny,)),
-                dma((ny,)),
-                dma((ny,)),
-                dma((ny,)),
+                dma((2, ny // 2 + 1, 2)),
+                dma((2, ny // 2 + 1, 2)),
             ],
             compiler_params=pltpu.CompilerParams(collective_id=0, has_side_effects=True),
             name="scan_and_ffn",

time: 69.9 us -> 69.8 us (level)
  the two profiles are of different devices: /device:TPU:392 before, /device:TPU:384 now
where the time goes in v2:
time: 69.8 us; the launch traced here: 69.6 us
  Pallas kernels  68.1 us (98%)
  local copies, waits for them, and re-layouts  1.47 us (2%)
    pallas_call x1, Pallas kernels, per_device(): pl.pallas_call(functools.partial(main_kernel, nz, ny), out_shape=jax.Shap...  61.1 us
    pallas_call x1, Pallas kernels, per_device(): pl.pallas_call(local_kernel, out_shape=(jax.ShapeDtypeStruct((2, 256, 128...  6.97 us
    unnamed x1, local copies, waits for them, and re-layouts  1.47 us

profile of v2, /device:TPU:384, one launch (start us, length us, event | category | flops | bytes accessed | tf_op | source)
XLA Modules:
  0.0 69.6 jit_solution(10100882272423114589)
XLA Ops:
  0.0 7.0 %local_terms.1 = (bf16[2,256,128]{2,1,0:T(8,128)(2,1)}, f32[2,128,128]{2,1,0:T(8,128)}, f32[2,128,128]{2,1,0:T(8,128)}, s32[2,4,32]{2,1,0:T(4,128)}) custom-call(bf16[256,128]{1,0:T(8,128)(2,1)} %bitcast.7, bf16[512,128]{1,0:T(8,128)(2,1)} %bitcast.5, bf16[512,128]{1,0:T(8,128)(2,1)} %bitcast.6, f32[2,2,128]{2,1,0:T(2,128)} %beta_ref.1, f32[2,128]{1,0:T(2,128)} %decay_ref.1, ...), custom_call_target="tpu_custom_call" | custom-call | tf_op jit(solution)/shard_map/local_terms/pallas_call | solution.py:637
  7.0 61.1 %scan_and_ffn.1 = bf16[128,256]{1,0:T(8,128)(2,1)} custom-call(s32[2,4,32]{2,1,0:T(4,128)} %get-tuple-element.9.inv_ref, bf16[2,256,128]{2,1,0:T(8,128)(2,1)} %get-tuple-element.10.tw_ref, f32[2,128,128]{2,1,0:T(8,128)} %get-tuple-element.11.qt_ref, f32[2,128,128]{2,1,0:T(8,128)} %get-tuple-element.12.lo_ref, bf16[128,256]{1,0:T(8,128)(2,1)} %res_ref.1, ...), custom_call_target="tpu_custom_call" | custom-call | tf_op jit(solution)/shard_map/scan_and_ffn/pallas_call | solution.py:657
  68.1 1.5 %copy.14 = bf16[128,256]{1,0:T(8,128)(2,1)} copy(bf16[128,256]{1,0:T(8,128)(2,1)} %scan_and_ffn.1) | data formatting | bytes 131072

commit v3 on v2

--- a/solution.py
+++ b/solution.py
@@ -11,6 +11,7 @@
 BF16 = jnp.bfloat16
 HIGHEST = lax.Precision.HIGHEST
 LANES_X = 4
+VMEM_LIMIT = 24 << 20
 MESH = pl.DeviceIdType.MESH
 
 
@@ -66,20 +67,19 @@
     return x
 
 
-def local_kernel(
-    q_ref, k_ref, v_ref, beta_ref, decay_ref, up_ref, down_ref, tw_ref, qt_ref, lo_ref, inv_ref
-):
+def inverse_table(index, kept):
+    lanes = iota((index.shape[0], 128), 1)
+    found = jnp.full(lanes.shape, kept, jnp.int32)
+    for j in range(kept):
+        found = jnp.where(index[:, j : j + 1] == lanes, j, found)
+    return found
+
+
+def local_terms(q_ref, k_ref, v_ref, beta_ref, decay_ref, tw_ref, qt_ref, lo_ref):
     tok = q_ref.shape[0] // 2
     span = 2 * tok
     heads = 2
     half = span // 2
-
-    for which, table in enumerate((up_ref, down_ref)):
-        for c in range(table.shape[0]):
-            for b in range(inv_ref.shape[2]):
-                inv_ref[which, c, b] = table.shape[1]
-            for j in range(table.shape[1]):
-                inv_ref[which, c, table[c, j]] = j
 
     kv = jnp.concatenate([k_ref[...], v_ref[...]], 1)
     q_all = q_ref[...]
@@ -176,16 +176,23 @@
 def main_kernel(
     nz,
     ny,
-    inv_ref,
-    tw_ref,
-    qt_ref,
-    lo_ref,
+    q_ref,
+    k_ref,
+    v_ref,
+    beta_ref,
+    decay_ref,
+    up_ref,
+    down_ref,
     res_ref,
     og_ref,
     fg_ref,
     up_hbm,
     down_hbm,
     out_ref,
+    qt_ref,
+    lo_ref,
+    table_v,
+    inv_ref,
     up_v,
     down_v,
     rx,
@@ -239,7 +246,7 @@
     barrier = pltpu.get_barrier_semaphore()
     peers = [(z * LANES_X + at_x(o), ten) for o in range(1, LANES_X)]
     peers += [(lax.rem(z + o, nz) * LANES_X + x, ten) for o in range(1, nz)]
-    peers += [(seq, at_y(o) * 2 + core) for o in range(1, ny)]
+    peers += [(seq, at_y(o) * 2 + core) for o in (1, 2, ny - 2, ny - 1)]
     peers += [(seq, partner)]
     for peer in peers:
         pl.semaphore_signal(barrier, inc=1, device_id=peer, device_id_type=MESH)
@@ -248,11 +255,15 @@
     load_down = pltpu.make_async_copy(down_hbm, down_v.at[:, pl.ds(0, kept)], wsem.at[1])
     load_up.start()
     load_down.start()
-    rx[x] = tw_ref[...]
     for c in range(groups):
         up_v[c, kept] = jnp.zeros(up_v.shape[2:], BF16)
         down_v[c, kept] = jnp.zeros(up_v.shape[2:], BF16)
     chain[...] = jnp.zeros_like(chain)
+    table_v[0:groups] = inverse_table(up_ref[...], kept)
+    table_v[groups : 2 * groups] = inverse_table(down_ref[...], kept)
+    load_table = pltpu.make_async_copy(table_v, inv_ref, wsem.at[2])
+    load_table.start()
+    local_terms(q_ref, k_ref, v_ref, beta_ref, decay_ref, rx.at[x], qt_ref, lo_ref)
     pl.semaphore_wait(barrier, len(peers))
 
     def remote(src, dst, send, recv, peer):
@@ -270,7 +281,7 @@
         h2, p2 = there // 2, lax.rem(there, 2)
         rows = pl.ds(pl.multiple_of(p2 * 64, 64), 192)
         return remote(
-            tw_ref.at[h2, rows],
+            rx.at[x, h2, rows],
             rx.at[x, h2, rows],
             a_send.at[o],
             a_recv.at[x],
@@ -284,10 +295,10 @@
         peer = (z * LANES_X + there, ten)
         return (
             remote(
-                tw_ref.at[h2, rows], rx.at[x, h2, rows], b_send.at[o], b_recv.at[x], peer
+                rx.at[x, h2, rows], rx.at[x, h2, rows], b_send.at[o], b_recv.at[x], peer
             ),
             remote(
-                tw_ref.at[1 - h2], rx.at[x, 1 - h2], c_send.at[o], c_recv.at[x], peer
+                rx.at[x, 1 - h2], rx.at[x, 1 - h2], c_send.at[o], c_recv.at[x], peer
             ),
         )
 
@@ -427,12 +438,15 @@
         if sent(i, d, p)
     ]
 
-    def neighbour(i):
-        return (seq, at_y(ways[i] + ny) * 2 + core)
+    hop = (0, 1, 2, 1, 2)
+
+    def across(i, d):
+        return (seq, at_y(ny + ways[i] * hop[d]) * 2 + core)
 
     def ring(i, d, p):
-        block = xg.at[at_y(ny - ways[i] * (d - 1)) * 2 + core, halves[p]]
-        return remote(block, block, g_send.at[i, d, p], g_recv.at[i, d, p], neighbour(i))
+        origin = 0 if d <= 2 else 2
+        block = xg.at[at_y(ny - ways[i] * origin) * 2 + core, halves[p]]
+        return remote(block, block, g_send.at[i, d, p], g_recv.at[i, d, p], across(i, d))
 
     def got(i, d, p):
         block = xg.at[at_y(ny - ways[i] * d) * 2 + core, halves[p]]
@@ -449,13 +463,15 @@
     def own_copy():
         return remote(xg.at[ten], xg.at[ten], o_sem.at[0], o_sem.at[1], (seq, partner))
 
-    for i, d, p in messages:
-        if d == 1:
-            ring(i, d, p).start()
+    for level in (2, 1):
+        for i, d, p in messages:
+            if d == level:
+                ring(i, d, p).start()
     own_copy().start()
 
     load_up.wait()
     load_down.wait()
+    load_table.wait()
 
     def absorb(slot, first, power):
         wide = xg[slot].astype(F32)
@@ -464,7 +480,7 @@
         weights = jnp.concatenate(
             [
                 jnp.concatenate(
-                    [up_v[c, inv_ref[0, c, 2 * slot + b]] for c in range(groups)], 1
+                    [up_v[c, inv_ref[c, 2 * slot + b]] for c in range(groups)], 1
                 )
                 for b in range(2)
             ],
@@ -483,26 +499,42 @@
     power = absorb(ten, True, jnp.zeros((xg.shape[1], 1), F32))
     remote(xg.at[partner], xg.at[partner], o_sem.at[0], o_sem.at[1], (seq, ten)).wait_recv()
     power = absorb(partner, False, power)
-    for d in range(1, reach + 1):
+
+    def take(d):
         for i, e, p in messages:
             if e == d:
                 got(i, d, p)
-                if d < reach and sent(i, d + 1, p):
-                    ring(i, d + 1, p).start()
+                if d == 2:
+                    for later in (4, 3):
+                        if sent(i, later, p):
+                            ring(i, later, p).start()
                 pass_on(i, d, p).start()
-        if d > 1:
-            for i, e, p in messages:
-                if e == d - 1:
-                    passed(i, e, p)
-            for where in blocks(d - 1):
-                power = absorb(where * 2 + 1 - core, False, power)
+
+    def near(d, power):
         for where in blocks(d):
             power = absorb(where * 2 + core, False, power)
-    for i, e, p in messages:
-        if e == reach:
-            passed(i, e, p)
-    for where in blocks(reach):
-        power = absorb(where * 2 + 1 - core, False, power)
+        return power
+
+    def far_side(d, power):
+        for i, e, p in messages:
+            if e == d:
+                passed(i, e, p)
+        for where in blocks(d):
+            power = absorb(where * 2 + 1 - core, False, power)
+        return power
+
+    take(2)
+    power = near(2, power)
+    take(1)
+    power = near(1, power)
+    power = far_side(2, power)
+    power = far_side(1, power)
+    take(3)
+    power = near(3, power)
+    take(4)
+    power = near(4, power)
+    power = far_side(3, power)
+    power = far_side(4, power)
 
     width = 256 * xg.shape[0]
     scale = lax.rsqrt(power / width + 1e-05)
@@ -512,7 +544,7 @@
         weights = jnp.concatenate(
             [
                 jnp.concatenate(
-                    [down_v[c, inv_ref[1, c, 2 * slot + b]] for b in range(2)], 1
+                    [down_v[c, inv_ref[groups + c, 2 * slot + b]] for b in range(2)], 1
                 )
                 for c in range(groups)
             ],
@@ -541,7 +573,7 @@
             rs.at[i, d, halves[p]],
             r_send.at[i, d, p],
             r_recv.at[i, d, p],
-            neighbour(i),
+            across(i, d),
         )
 
     def m_got(i, d, p):
@@ -554,35 +586,40 @@
     def rows_of(value, p):
         return value[p * rows_dev : (p + 1) * rows_dev]
 
-    def offer_level(d):
-        for off in (d, -d) if d else (0,):
-            offer(off)
-
-    offer(reach)
-    offer_level(reach - 1)
-    far = pair_sum(reach)
+    def ship(i, d, p, value):
+        psum[i, d, halves[p]] = value.astype(BF16)
+        m_copy(i, d, p).start()
+
+    def ship_both(d):
+        for i in range(2):
+            value = pair_sum(ways[i] * d)
+            for p in range(2):
+                ship(i, d, p, rows_of(value, p))
+
+    for off in (4, 3, -3):
+        offer(off)
+    far = pair_sum(4)
     for i in range(2):
-        psum[i, reach, halves[i]] = rows_of(far, i).astype(BF16)
-        m_copy(i, reach, i).start()
-    for d in range(reach - 1, 0, -1):
-        offer_level(d - 1)
-        sums = [pair_sum(d), pair_sum(-d)]
-        for fresh in (True, False):
-            for p in range(2):
-                for i in range(2):
-                    if sent(i, d + 1, p) == fresh:
-                        continue
-                    value = rows_of(sums[i], p)
-                    if not fresh:
-                        value = value + m_got(i, d + 1, p)
-                    psum[i, d, halves[p]] = value.astype(BF16)
-                    m_copy(i, d, p).start()
+        ship(i, 4, i, rows_of(far, i))
+    for off in (2, -2):
+        offer(off)
+    ship_both(3)
+    for off in (1, -1, 0):
+        offer(off)
+    ship_both(1)
+    sums = [pair_sum(2), pair_sum(-2)]
     total = pair_sum(0) + xg[ten].astype(F32)
     for p in range(2):
+        for i in range(2):
+            value = rows_of(sums[i], p) + m_got(i, 3, p)
+            if sent(i, 4, p):
+                value = value + m_got(i, 4, p)
+            ship(i, 2, p, value)
+    for p in range(2):
         value = rows_of(total, p)
-        for i in range(2):
-            if sent(i, 1, p):
-                value = value + m_got(i, 1, p)
+        for d in (1, 2):
+            for i in range(2):
+                value = value + m_got(i, d, p)
         out_ref[halves[p], :] = value.astype(BF16)
 
     for o in range(1, LANES_X):
@@ -613,7 +650,6 @@
     nseq, nten = mesh.shape["seq"], mesh.shape["tensor"]
     nz, ny = nseq // LANES_X, nten // 2
     vmem = pl.BlockSpec(memory_space=pltpu.VMEM)
-    smem = pl.BlockSpec(memory_space=pltpu.SMEM)
     anywhere = pl.BlockSpec(memory_space=pl.ANY)
     dma = pltpu.SemaphoreType.DMA
 
@@ -633,33 +669,16 @@
     ):
         tok = queries.shape[0]
         groups, kept = up_index.shape
-        tiles = 2 * nten
-        tw, qt, lo, inv = pl.pallas_call(
-            local_kernel,
-            out_shape=(
-                jax.ShapeDtypeStruct((2, 256, 128), BF16),
-                jax.ShapeDtypeStruct((2, tok, 128), F32),
-                jax.ShapeDtypeStruct((2, tok, 128), F32),
-                jax.ShapeDtypeStruct((2, groups, tiles), jnp.int32),
-            ),
-            in_specs=[vmem] * 5 + [smem] * 2,
-            out_specs=(vmem, vmem, vmem, smem),
-            name="local_terms",
-        )(
-            queries.reshape(2 * tok, 128),
-            keys.reshape(4 * tok, 128),
-            values.reshape(4 * tok, 128),
-            beta,
-            decay,
-            up_index,
-            down_index,
-        )
         return pl.pallas_call(
             functools.partial(main_kernel, nz, ny),
             out_shape=jax.ShapeDtypeStruct((tok, 256), BF16),
-            in_specs=[smem] + [vmem] * 6 + [anywhere] * 2,
+            in_specs=[vmem] * 10 + [anywhere] * 2,
             out_specs=vmem,
             scratch_shapes=[
+                pltpu.VMEM((2, tok, 128), F32),
+                pltpu.VMEM((2, tok, 128), F32),
+                pltpu.VMEM((2 * groups, 128), jnp.int32),
+                pltpu.SMEM((2 * groups, 128), jnp.int32),
                 pltpu.VMEM((groups, kept + 1, 128, 128), BF16),
                 pltpu.VMEM((groups, kept + 1, 128, 128), BF16),
                 pltpu.VMEM((LANES_X, 2, 256, 128), BF16),
@@ -675,7 +694,7 @@
                 pltpu.VMEM((ny, tok, 256), BF16),
                 pltpu.VMEM((2, ny // 2 + 1, tok, 256), BF16),
                 pltpu.VMEM((2, ny // 2 + 1, tok, 256), BF16),
-                dma((2,)),
+                dma((3,)),
                 dma((LANES_X,)),
                 dma((LANES_X,)),
                 dma((LANES_X,)),
@@ -696,13 +715,18 @@
                 dma((2, ny // 2 + 1, 2)),
                 dma((2, ny // 2 + 1, 2)),
             ],
-            compiler_params=pltpu.CompilerParams(collective_id=0, has_side_effects=True),
-            name="scan_and_ffn",
+            compiler_params=pltpu.CompilerParams(
+                collective_id=0, has_side_effects=True, vmem_limit_bytes=VMEM_LIMIT
+            ),
+            name="layer",
         )(
-            inv,
-            tw,
-            qt,
-            lo,
+            queries.reshape(2 * tok, 128),
+            keys.reshape(4 * tok, 128),
+            values.reshape(4 * tok, 128),
+            beta,
+            decay,
+            up_index,
+            down_index,
             residual,
             out_gain.reshape(1, 128),
             ffn_gain.reshape(nten, 1, 256),

time: 69.8 us -> 62.2 us (0.89)
  Pallas kernels: 68.1 us -> 50.4 us
  local copies, waits for them, and re-layouts: 1.47 us -> 11.4 us
    pallas_call x1, Pallas kernels: 61.1 us -> 50.4 us  [per_device(): pl.pallas_call(functools.partial(main_kernel, nz, ny), out_shape=jax.Shap...]
    unnamed x1 -> x25, local copies, waits for them, and re-layouts: 1.47 us -> 11.4 us
    pallas_call x1 -> x0, Pallas kernels: 6.97 us -> none  [per_device(): pl.pallas_call(local_kernel, out_shape=(jax.ShapeDtypeStruct((2, 256, 128...]
where the time goes in v3:
time: 62.2 us; the launch traced here: 61.8 us
  Pallas kernels  50.4 us (81%)
  local copies, waits for them, and re-layouts  11.4 us (18%)
    pallas_call x1, Pallas kernels, per_device(): pl.pallas_call(functools.partial(main_kernel, nz, ny), out_shape=jax.Shap...  50.4 us
    unnamed x25, local copies, waits for them, and re-layouts  11.4 us

profile of v3, /device:TPU:384, one launch (start us, length us, event | category | flops | bytes accessed | tf_op | source)
XLA Modules:
  0.0 61.8 jit_solution(12048346286546171191)
XLA Ops:
  0.0 0.0 copy-start
  0.0 1.6 %copy-done = bf16[4,16,128,128]{3,2,1,0:T(8,128)(2,1)S(1)} copy-done((bf16[4,16,128,128]{3,2,1,0:T(8,128)(2,1)S(1)}, bf16[4,16,128,128]{3,2,1,0:T(8,128)(2,1)}, u32[]{:S(2)}) %copy-start) | copy-done | bytes 2097176
  1.6 0.0 copy-start.1
  1.6 1.6 %copy-done.1 = bf16[4,16,128,128]{3,2,1,0:T(8,128)(2,1)S(1)} copy-done((bf16[4,16,128,128]{3,2,1,0:T(8,128)(2,1)S(1)}, bf16[4,16,128,128]{3,2,1,0:T(8,128)(2,1)}, u32[]{:S(2)}) %copy-start.1) | copy-done | bytes 2097176
  3.2 0.0 copy-start.2
  3.2 0.9 %copy-done.2 = bf16[2,128,2,128]{3,2,1,0:T(2,128)(2,1)S(1)} copy-done((bf16[2,128,2,128]{3,2,1,0:T(2,128)(2,1)S(1)}, bf16[2,128,2,128]{3,2,1,0:T(2,128)(2,1)}, u32[]{:S(2)}) %copy-start.2) | copy-done | bytes 131096
  4.1 0.0 copy-start.3
  4.1 0.9 %copy-done.3 = bf16[2,128,2,128]{3,2,1,0:T(2,128)(2,1)S(1)} copy-done((bf16[2,128,2,128]{3,2,1,0:T(2,128)(2,1)S(1)}, bf16[2,128,2,128]{3,2,1,0:T(2,128)(2,1)}, u32[]{:S(2)}) %copy-start.3) | copy-done | bytes 131096
  5.0 0.0 copy-start.4
  5.0 0.8 %copy-done.4 = bf16[128,2,128]{2,1,0:T(2,128)(2,1)S(1)} copy-done((bf16[128,2,128]{2,1,0:T(2,128)(2,1)S(1)}, bf16[128,2,128]{2,1,0:T(2,128)(2,1)}, u32[]{:S(2)}) %copy-start.4) | copy-done | bytes 65560
  5.8 0.0 copy-start.5
  5.8 0.8 %copy-done.5 = bf16[128,256]{1,0:T(8,128)(2,1)S(1)} copy-done((bf16[128,256]{1,0:T(8,128)(2,1)S(1)}, bf16[128,256]{1,0:T(8,128)(2,1)}, u32[]{:S(2)}) %copy-start.5) | copy-done | bytes 65560
  6.7 0.0 copy-start.6
  6.7 0.7 %copy-done.6 = f32[4096]{0:T(1024)S(1)} copy-done((f32[4096]{0:T(1024)S(1)}, f32[4096]{0:T(1024)}, u32[]{:S(2)}) %copy-start.6) | copy-done | bytes 16408
  7.4 0.0 copy-start.7
  7.4 0.7 %copy-done.7 = f32[2,2,128]{2,1,0:T(2,128)S(1)} copy-done((f32[2,2,128]{2,1,0:T(2,128)S(1)}, f32[2,2,128]{2,1,0:T(2,128)}, u32[]{:S(2)}) %copy-start.7) | copy-done | bytes 2072
  8.1 0.0 copy-start.8
  8.1 0.7 %copy-done.8 = s32[4,16]{1,0:T(4,128)S(1)} copy-done((s32[4,16]{1,0:T(4,128)S(1)}, s32[4,16]{1,0:T(4,128)}, u32[]{:S(2)}) %copy-start.8) | copy-done | bytes 280
  8.8 0.0 copy-start.9
  8.8 0.7 %copy-done.9 = s32[4,16]{1,0:T(4,128)S(1)} copy-done((s32[4,16]{1,0:T(4,128)S(1)}, s32[4,16]{1,0:T(4,128)}, u32[]{:S(2)}) %copy-start.9) | copy-done | bytes 280
  9.4 0.0 copy-start.10
  9.4 0.7 %copy-done.10 = f32[2,128]{1,0:T(2,128)S(1)} copy-done((f32[2,128]{1,0:T(2,128)S(1)}, f32[2,128]{1,0:T(2,128)}, u32[]{:S(2)}) %copy-start.10) | copy-done | bytes 1048
  10.1 0.0 copy-start.11
  10.1 0.7 %copy-done.11 = f32[128]{0:T(128)S(1)} copy-done((f32[128]{0:T(128)S(1)}, f32[128]{0:T(128)}, u32[]{:S(2)}) %copy-start.11) | copy-done | bytes 536
  10.8 50.4 %layer.1 = bf16[128,256]{1,0:T(8,128)(2,1)S(1)} custom-call(bf16[256,128]{1,0:T(8,128)(2,1)S(1)} %bitcast.7, bf16[512,128]{1,0:T(8,128)(2,1)S(1)} %bitcast.5, bf16[512,128]{1,0:T(8,128)(2,1)S(1)} %bitcast.6, f32[2,2,128]{2,1,0:T(2,128)S(1)} %copy-done.7, f32[2,128]{1,0:T(2,128)S(1)} %copy-done.10, s32[4,16]{1,0:T(4,128)S(1)} %copy-done.8, ...), custom_call_target="tpu_custom_call" | custom-call | tf_op jit(solution)/shard_map/layer/pallas_call | solution.py:672
  61.1 0.6 %copy.14 = bf16[128,256]{1,0:T(8,128)(2,1)} copy(bf16[128,256]{1,0:T(8,128)(2,1)S(1)} %layer.1) | data formatting | bytes 131072
Async XLA Ops:
  0.0 1.6 %copy-start = (bf16[4,16,128,128]{3,2,1,0:T(8,128)(2,1)S(1)}, bf16[4,16,128,128]{3,2,1,0:T(8,128)(2,1)}, u32[]{:S(2)}) copy-start(bf16[4,16,128,128]{3,2,1,0:T(8,128)(2,1)} %up_hbm.1) | copy-start | bytes 6291460
  1.6 1.6 %copy-start.1 = (bf16[4,16,128,128]{3,2,1,0:T(8,128)(2,1)S(1)}, bf16[4,16,128,128]{3,2,1,0:T(8,128)(2,1)}, u32[]{:S(2)}) copy-start(bf16[4,16,128,128]{3,2,1,0:T(8,128)(2,1)} %down_hbm.1) | copy-start | bytes 6291460
  3.2 0.9 %copy-start.2 = (bf16[2,128,2,128]{3,2,1,0:T(2,128)(2,1)S(1)}, bf16[2,128,2,128]{3,2,1,0:T(2,128)(2,1)}, u32[]{:S(2)}) copy-start(bf16[2,128,2,128]{3,2,1,0:T(2,128)(2,1)} %param.13) | copy-start | bytes 393220
  4.1 0.9 %copy-start.3 = (bf16[2,128,2,128]{3,2,1,0:T(2,128)(2,1)S(1)}, bf16[2,128,2,128]{3,2,1,0:T(2,128)(2,1)}, u32[]{:S(2)}) copy-start(bf16[2,128,2,128]{3,2,1,0:T(2,128)(2,1)} %param.14) | copy-start | bytes 393220
  5.0 0.8 %copy-start.4 = (bf16[128,2,128]{2,1,0:T(2,128)(2,1)S(1)}, bf16[128,2,128]{2,1,0:T(2,128)(2,1)}, u32[]{:S(2)}) copy-start(bf16[128,2,128]{2,1,0:T(2,128)(2,1)} %param.12) | copy-start | bytes 196612
  5.8 0.8 %copy-start.5 = (bf16[128,256]{1,0:T(8,128)(2,1)S(1)}, bf16[128,256]{1,0:T(8,128)(2,1)}, u32[]{:S(2)}) copy-start(bf16[128,256]{1,0:T(8,128)(2,1)} %res_ref.1) | copy-start | bytes 196612
  6.7 0.7 %copy-start.6 = (f32[4096]{0:T(1024)S(1)}, f32[4096]{0:T(1024)}, u32[]{:S(2)}) copy-start(f32[4096]{0:T(1024)} %param.19) | copy-start | bytes 49156
  7.4 0.7 %copy-start.7 = (f32[2,2,128]{2,1,0:T(2,128)S(1)}, f32[2,2,128]{2,1,0:T(2,128)}, u32[]{:S(2)}) copy-start(f32[2,2,128]{2,1,0:T(2,128)} %beta_ref.1) | copy-start | bytes 6148
  8.1 0.7 %copy-start.8 = (s32[4,16]{1,0:T(4,128)S(1)}, s32[4,16]{1,0:T(4,128)}, u32[]{:S(2)}) copy-start(s32[4,16]{1,0:T(4,128)} %up_ref.1) | copy-start | bytes 772
  8.8 0.7 %copy-start.9 = (s32[4,16]{1,0:T(4,128)S(1)}, s32[4,16]{1,0:T(4,128)}, u32[]{:S(2)}) copy-start(s32[4,16]{1,0:T(4,128)} %down_ref.1) | copy-start | bytes 772
  9.4 0.7 %copy-start.10 = (f32[2,128]{1,0:T(2,128)S(1)}, f32[2,128]{1,0:T(2,128)}, u32[]{:S(2)}) copy-start(f32[2,128]{1,0:T(2,128)} %decay_ref.1) | copy-start | bytes 3076
  10.1 0.7 %copy-start.11 = (f32[128]{0:T(128)S(1)}, f32[128]{0:T(128)}, u32[]{:S(2)}) copy-start(f32[128]{0:T(128)} %param.17) | copy-start | bytes 1540

commit v4 on v3

--- a/solution.py
+++ b/solution.py
@@ -176,6 +176,19 @@
 def main_kernel(
     nz,
     ny,
+    q_in,
+    k_in,
+    v_in,
+    beta_in,
+    decay_in,
+    up_in,
+    down_in,
+    res_in,
+    og_in,
+    fg_in,
+    up_hbm,
+    down_hbm,
+    out_ref,
     q_ref,
     k_ref,
     v_ref,
@@ -186,9 +199,7 @@
     res_ref,
     og_ref,
     fg_ref,
-    up_hbm,
-    down_hbm,
-    out_ref,
+    l_sem,
     qt_ref,
     lo_ref,
     table_v,
@@ -251,6 +262,23 @@
     for peer in peers:
         pl.semaphore_signal(barrier, inc=1, device_id=peer, device_id_type=MESH)
 
+    inputs = (
+        (k_in, k_ref),
+        (v_in, v_ref),
+        (q_in, q_ref),
+        (beta_in, beta_ref),
+        (decay_in, decay_ref),
+        (up_in, up_ref),
+        (down_in, down_ref),
+        (res_in, res_ref),
+        (og_in, og_ref),
+        (fg_in, fg_ref),
+    )
+    loads = [
+        pltpu.make_async_copy(here, there, l_sem.at[n]) for n, (here, there) in enumerate(inputs)
+    ]
+    for load in loads:
+        load.start()
     load_up = pltpu.make_async_copy(up_hbm, up_v.at[:, pl.ds(0, kept)], wsem.at[0])
     load_down = pltpu.make_async_copy(down_hbm, down_v.at[:, pl.ds(0, kept)], wsem.at[1])
     load_up.start()
@@ -259,6 +287,8 @@
         up_v[c, kept] = jnp.zeros(up_v.shape[2:], BF16)
         down_v[c, kept] = jnp.zeros(up_v.shape[2:], BF16)
     chain[...] = jnp.zeros_like(chain)
+    for load in loads:
+        load.wait()
     table_v[0:groups] = inverse_table(up_ref[...], kept)
     table_v[groups : 2 * groups] = inverse_table(down_ref[...], kept)
     load_table = pltpu.make_async_copy(table_v, inv_ref, wsem.at[2])
@@ -650,7 +680,7 @@
     nseq, nten = mesh.shape["seq"], mesh.shape["tensor"]
     nz, ny = nseq // LANES_X, nten // 2
     vmem = pl.BlockSpec(memory_space=pltpu.VMEM)
-    anywhere = pl.BlockSpec(memory_space=pl.ANY)
+    hbm = pl.BlockSpec(memory_space=pltpu.HBM)
     dma = pltpu.SemaphoreType.DMA
 
     def per_device(
@@ -672,9 +702,20 @@
         return pl.pallas_call(
             functools.partial(main_kernel, nz, ny),
             out_shape=jax.ShapeDtypeStruct((tok, 256), BF16),
-            in_specs=[vmem] * 10 + [anywhere] * 2,
+            in_specs=[hbm] * 12,
             out_specs=vmem,
             scratch_shapes=[
+                pltpu.VMEM((2 * tok, 128), BF16),
+                pltpu.VMEM((4 * tok, 128), BF16),
+                pltpu.VMEM((4 * tok, 128), BF16),
+                pltpu.VMEM((2, 2, tok), F32),
+                pltpu.VMEM((2, tok), F32),
+                pltpu.VMEM((groups, kept), jnp.int32),
+                pltpu.VMEM((groups, kept), jnp.int32),
+                pltpu.VMEM((tok, 256), BF16),
+                pltpu.VMEM((1, 128), F32),
+                pltpu.VMEM((nten, 1, 256), F32),
+                dma((10,)),
                 pltpu.VMEM((2, tok, 128), F32),
                 pltpu.VMEM((2, tok, 128), F32),
                 pltpu.VMEM((2 * groups, 128), jnp.int32),
@@ -719,7 +760,7 @@
                 collective_id=0, has_side_effects=True, vmem_limit_bytes=VMEM_LIMIT
             ),
             name="layer",
-        )(
+        )(*(pltpu.with_memory_space_constraint(a, pltpu.HBM) for a in (
             queries.reshape(2 * tok, 128),
             keys.reshape(4 * tok, 128),
             values.reshape(4 * tok, 128),
@@ -732,7 +773,7 @@
             ffn_gain.reshape(nten, 1, 256),
             up_blocks,
             down_kept_tiles,
-        )
+        )))
 
     placed = (
         P("seq", "tensor", None),

time: 62.2 us -> 52.4 us (0.84)
  local copies, waits for them, and re-layouts: 11.4 us -> 0.63 us
  Pallas kernels: 50.4 us -> 51.7 us
    unnamed x25 -> x1, local copies, waits for them, and re-layouts: 11.4 us -> 0.63 us
    pallas_call x1, Pallas kernels: 50.4 us -> 51.7 us  [per_device(): pl.pallas_call(functools.partial(main_kernel, nz, ny), out_shape=jax.Shap...]
where the time goes in v4:
time: 52.4 us; the launch traced here: 52.3 us
  Pallas kernels  51.7 us (99%)
  local copies, waits for them, and re-layouts  0.63 us (1%)
    pallas_call x1, Pallas kernels, per_device(): pl.pallas_call(functools.partial(main_kernel, nz, ny), out_shape=jax.Shap...  51.7 us

profile of v4, /device:TPU:384, one launch (start us, length us, event | category | flops | bytes accessed | tf_op | source)
XLA Modules:
  0.0 52.3 jit_solution(15856225120816869308)
XLA Ops:
  0.0 51.7 %layer.1 = bf16[128,256]{1,0:T(8,128)(2,1)S(1)} custom-call(bf16[256,128]{1,0:T(8,128)(2,1)} %bitcast.7, bf16[512,128]{1,0:T(8,128)(2,1)} %bitcast.5, bf16[512,128]{1,0:T(8,128)(2,1)} %bitcast.6, f32[2,2,128]{2,1,0:T(2,128)} %beta_in.1, f32[2,128]{1,0:T(2,128)} %decay_in.1, s32[4,16]{1,0:T(4,128)} %up_in.1, s32[4,16]{1,0:T(4,128)} %down_in.1, ...), custom_call_target="tpu_custom_call" | custom-call | tf_op jit(solution)/shard_map/layer/pallas_call | solution.py:702
  51.7 0.6 %copy.14 = bf16[128,256]{1,0:T(8,128)(2,1)} copy(bf16[128,256]{1,0:T(8,128)(2,1)S(1)} %layer.1) | data formatting | bytes 131072

commit v5 on v4

--- a/solution.py
+++ b/solution.py
@@ -82,20 +82,27 @@
     half = span // 2
 
     kv = jnp.concatenate([k_ref[...], v_ref[...]], 1)
-    q_all = q_ref[...]
     small = jnp.concatenate(
         [decay_ref[...], beta_ref[0], beta_ref[1], jnp.zeros((2, tok), F32)], 0
     )
+    s1 = small.astype(BF16)
+    rest = small - s1.astype(F32)
+    s2 = rest.astype(BF16)
+    s3 = (rest - s2.astype(F32)).astype(BF16)
+    parts = jnp.concatenate([s1, s2, s3, jnp.zeros_like(s1)], 0)
     m_at, t_at = iota((span, tok), 0), iota((span, tok), 1)
-    upto = (t_at <= (m_at >> 1)).astype(F32)
-    first = ((t_at == (m_at >> 1)) & ((m_at & 1) == 0)).astype(F32)
-    second = ((t_at == (m_at >> 1)) & ((m_at & 1) == 1)).astype(F32)
-    upto_tok = (iota((tok, tok), 1) <= iota((tok, tok), 0)).astype(F32)
-    run_col = dot(upto, small, (1, 1), HIGHEST)
-    run_row = dot(small, upto, (1, 1), HIGHEST)
-    tok_col = dot(upto_tok, small, (1, 1), HIGHEST)
-    one_col, two_col = dot(first, small, (1, 1), HIGHEST), dot(second, small, (1, 1), HIGHEST)
-    one_row, two_row = dot(small, first, (1, 1), HIGHEST), dot(small, second, (1, 1), HIGHEST)
+    upto = t_at <= (m_at >> 1)
+    first = (t_at == (m_at >> 1)) & ((m_at & 1) == 0)
+    second = (t_at == (m_at >> 1)) & ((m_at & 1) == 1)
+    upto_tok = iota((tok, tok), 1) <= iota((tok, tok), 0)
+    picks = jnp.concatenate([e.astype(BF16) for e in (upto, first, second, upto_tok)], 0)
+    cols3 = dot(picks, parts, (1, 1))
+    col = cols3[:, 0:8] + cols3[:, 8:16] + cols3[:, 16:24]
+    rows3 = dot(parts, picks, (1, 1))
+    row = rows3[0:8] + rows3[8:16] + rows3[16:24]
+    run_col, one_col, two_col = col[:span], col[span : 2 * span], col[2 * span : 3 * span]
+    tok_col = col[3 * span :]
+    run_row, one_row, two_row = row[:, :span], row[:, span : 2 * span], row[:, 2 * span : 3 * span]
 
     rows, cols = iota((span, span), 0), iota((span, span), 1)
     below = cols < rows
@@ -113,7 +120,6 @@
         pick = (column == place + h).astype(BF16)
         both = dot(pick, kv).astype(BF16)
         k, v = both[:, :128], both[:, 128:]
-        q = dot((q_column == q_place + h).astype(BF16), q_all)
         gram = dot(k, k, (1, 1))
         diag = jnp.where(same, gram, 0.0)
         rk_col = lax.rsqrt(jnp.sum(diag, 1, keepdims=True) + 1e-06)
@@ -123,14 +129,15 @@
         beta_r = one_row[2 + h : 3 + h, :] + two_row[4 + h : 5 + h, :]
         fade = jnp.exp(jnp.where(below, run_c - run_r, 0.0))
         low = jnp.where(below, (beta_c * rk_col) * fade * gram * rk_row, 0.0)
-        keep.append((k, v, q, rk_col, rk_row, run_c, run_r, beta_r, low))
+        keep.append((k, v, rk_col, rk_row, run_c, run_r, beta_r, low))
         lowers += [low[:half, :half], low[half:, half:]]
 
     inverses = unit_lower_inverse(lowers)
-    mids = [mm3(keep[h][8][half:, :half], inverses[2 * h]) for h in range(heads)]
+    mids = [mm3(keep[h][7][half:, :half], inverses[2 * h]) for h in range(heads)]
     crosses = [mm3(inverses[2 * h + 1], mids[h]) for h in range(heads)]
+    left = []
     for h in range(heads):
-        k, v, q, rk_col, rk_row, run_c, run_r, beta_r, low = keep[h]
+        k, v, rk_col, rk_row, run_c, run_r, beta_r, low = keep[h]
         a = jnp.concatenate(
             [
                 jnp.concatenate([inverses[2 * h], jnp.zeros((half, half), F32)], 1),
@@ -153,17 +160,25 @@
         tw_ref[h, 0:64, :] = write_t[:64].astype(BF16)
         tw_ref[h, 64:192, :] = trans.astype(BF16)
         tw_ref[h, 192:256, :] = write_t[64:].astype(BF16)
-        tok_run = tok_col[:, h : h + 1]
-        rq = lax.rsqrt(jnp.sum(q * q, 1, keepdims=True) + 1e-06)
-        qk = dot(q.astype(BF16), k, (1, 1))
-        mixing = jnp.where(
-            reach, jnp.exp(jnp.where(reach, tok_run - run_r, 0.0)) * qk * rq * rk_row, 0.0
-        )
-        mh, ml = split(mixing)
-        bh, bl = split(jnp.concatenate([w, u], 1))
-        mixed = dot(mh, bh) + dot(ml, bh) + dot(mh, bl)
-        qt_ref[h] = (jnp.exp(tok_run) * rq) * q - mixed[:, :128]
-        lo_ref[h] = mixed[:, 128:]
+        left.append((k, u, w, rk_row, run_r, tok_col[:, h : h + 1]))
+
+    def queries():
+        q_all = q_ref[...]
+        for h in range(heads):
+            k, u, w, rk_row, run_r, tok_run = left[h]
+            q = dot((q_column == q_place + h).astype(BF16), q_all)
+            rq = lax.rsqrt(jnp.sum(q * q, 1, keepdims=True) + 1e-06)
+            qk = dot(q.astype(BF16), k, (1, 1))
+            mixing = jnp.where(
+                reach, jnp.exp(jnp.where(reach, tok_run - run_r, 0.0)) * qk * rq * rk_row, 0.0
+            )
+            mh, ml = split(mixing)
+            bh, bl = split(jnp.concatenate([w, u], 1))
+            mixed = dot(mh, bh) + dot(ml, bh) + dot(mh, bl)
+            qt_ref[h] = (jnp.exp(tok_run) * rq) * q - mixed[:, :128]
+            lo_ref[h] = mixed[:, 128:]
+
+    return queries
 
 
 def chain_step(state, trans, write):
@@ -210,6 +225,9 @@
     zmsg,
     rz,
     chain,
+    since,
+    before_t,
+    before_w,
     pmsg,
     rp,
     xg,
@@ -283,17 +301,9 @@
     load_down = pltpu.make_async_copy(down_hbm, down_v.at[:, pl.ds(0, kept)], wsem.at[1])
     load_up.start()
     load_down.start()
-    for c in range(groups):
-        up_v[c, kept] = jnp.zeros(up_v.shape[2:], BF16)
-        down_v[c, kept] = jnp.zeros(up_v.shape[2:], BF16)
-    chain[...] = jnp.zeros_like(chain)
     for load in loads:
         load.wait()
-    table_v[0:groups] = inverse_table(up_ref[...], kept)
-    table_v[groups : 2 * groups] = inverse_table(down_ref[...], kept)
-    load_table = pltpu.make_async_copy(table_v, inv_ref, wsem.at[2])
-    load_table.start()
-    local_terms(q_ref, k_ref, v_ref, beta_ref, decay_ref, rx.at[x], qt_ref, lo_ref)
+    queries = local_terms(q_ref, k_ref, v_ref, beta_ref, decay_ref, rx.at[x], qt_ref, lo_ref)
     pl.semaphore_wait(barrier, len(peers))
 
     def remote(src, dst, send, recv, peer):
@@ -306,10 +316,16 @@
             device_id_type=MESH,
         )
 
-    def a_copy(o):
+    w_rows = pl.ds(pl.multiple_of(part * 192, 64), 64)
+    my_rows = pl.ds(pl.multiple_of(part * 64, 64), 192)
+
+    def a_copy(o, only_write):
         there = at_x(o)
         h2, p2 = there // 2, lax.rem(there, 2)
-        rows = pl.ds(pl.multiple_of(p2 * 64, 64), 192)
+        if only_write:
+            rows = pl.ds(pl.multiple_of(p2 * 192, 64), 64)
+        else:
+            rows = pl.ds(pl.multiple_of(p2 * 64, 64), 192)
         return remote(
             rx.at[x, h2, rows],
             rx.at[x, h2, rows],
@@ -317,6 +333,35 @@
             a_recv.at[x],
             (z * LANES_X + there, ten),
         )
+
+    def on_first(act_on):
+        @pl.when(seq == 0)
+        def _():
+            act_on(True)
+
+        @pl.when(seq != 0)
+        def _():
+            act_on(False)
+
+    def a_wait(i):
+        def wait(only_write):
+            block = rx.at[i, head, w_rows if only_write else my_rows]
+            remote(block, block, a_send.at[0], a_recv.at[i], (seq, ten)).wait_recv()
+
+        @pl.when(i != x)
+        def _():
+            if i == 0:
+
+                @pl.when(z == 0)
+                def _():
+                    wait(True)
+                    rx[0, head, 64:192] = jnp.zeros((128, 128), BF16)
+
+                @pl.when(z != 0)
+                def _():
+                    wait(False)
+            else:
+                wait(False)
 
     def b_copies(o):
         there = at_x(o)
@@ -333,45 +378,68 @@
         )
 
     for o in (2, 1, 3):
-        a_copy(o).start()
-    my_rows = pl.ds(pl.multiple_of(part * 64, 64), 192)
-    for o in (1, 3, 2):
-        source = at_x(o)
-        remote(
-            rx.at[source, head, my_rows],
-            rx.at[source, head, my_rows],
-            a_send.at[o],
-            a_recv.at[source],
-            (seq, ten),
-        ).wait_recv()
-
-    w_rows = pl.ds(pl.multiple_of(part * 192, 64), 64)
-    ts = [rx[i, head, pl.ds(64, 128)] for i in range(LANES_X)]
-    ws = [rx[i, head, w_rows] for i in range(LANES_X)]
-    t10, t32 = dot(ts[1], ts[0]), dot(ts[3], ts[2])
-    w10 = dot(ws[0], ts[1], (1, 1)) + ws[1].astype(F32)
-    w32 = dot(ws[2], ts[3], (1, 1)) + ws[3].astype(F32)
-    zmsg[64:192] = mm3(t32, t10).astype(BF16)
-    th, tl = split(t32)
-    wh, wl = split(w10)
-    mixed = dot(jnp.concatenate([wh, wl], 0), th, (1, 1))
-    w_all = mixed[:64] + mixed[64:] + dot(wh, tl, (1, 1)) + w32
-    zmsg[0:64] = w_all.astype(BF16)
-
-    def z_copy(o):
+        on_first(lambda only_write: a_copy(o, only_write).start())
+
+    chain[...] = jnp.zeros_like(chain)
+    eye = (iota((128, 128), 0) == iota((128, 128), 1)).astype(F32)
+    since[...] = eye
+    for h in range(2):
+        before_t[h] = eye
+        before_w[h] = jnp.zeros((128, 128), F32)
+    table_v[0:groups] = inverse_table(up_ref[...], kept)
+    table_v[groups : 2 * groups] = inverse_table(down_ref[...], kept)
+    load_table = pltpu.make_async_copy(table_v, inv_ref, wsem.at[2])
+    load_table.start()
+    for c in range(groups):
+        up_v[c, kept] = jnp.zeros(up_v.shape[2:], BF16)
+        down_v[c, kept] = jnp.zeros(up_v.shape[2:], BF16)
+    queries()
+
+    def apply(write, trans):
+        high, low = split(trans)
+        return dot(write, high, (1, 1)) + dot(write, low, (1, 1))
+
+    def extend(trans, earlier):
+        high, low = split(trans)
+        both = dot(jnp.concatenate([high, low], 0), earlier)
+        return both[:128] + both[128:]
+
+    for i in (3, 2, 1):
+        a_wait(i)
+    ts = [rx[i, head, pl.ds(64, 128)] for i in range(1, LANES_X)]
+    ws = [rx[i, head, w_rows] for i in range(1, LANES_X)]
+    t32 = dot(ts[2], ts[1])
+    w32 = dot(ws[1], ts[2], (1, 1)) + ws[2].astype(F32)
+    t321 = extend(t32, ts[0])
+    w321 = apply(ws[0], t32) + w32
+    a_wait(0)
+    zmsg[0:64] = (apply(rx[0, head, w_rows], t321) + w321).astype(BF16)
+    zmsg[64:192] = extend(t321, rx[0, head, pl.ds(64, 128)]).astype(BF16)
+
+    def z_copy(o, only_write):
+        rows = pl.ds(0, 64 if only_write else 192)
         return remote(
-            zmsg,
-            rz.at[z],
+            zmsg.at[rows],
+            rz.at[z, rows],
             z_send.at[o],
             z_recv.at[z],
             ((z + o) * LANES_X + x, ten),
         )
 
+    def on_first_group(act_on):
+        @pl.when(z == 0)
+        def _():
+            act_on(True)
+
+        @pl.when(z != 0)
+        def _():
+            act_on(False)
+
     for o in range(1, nz):
 
         @pl.when(z + o < nz)
         def _():
-            z_copy(o).start()
+            on_first_group(lambda only_write: z_copy(o, only_write).start())
 
     for o in range(1, LANES_X):
 
@@ -380,34 +448,6 @@
             for one in b_copies(o):
                 one.start()
 
-    for i in range(nz - 1):
-
-        @pl.when(i < z)
-        def _():
-            remote(
-                rz.at[i], rz.at[i], z_send.at[0], z_recv.at[i], (seq, ten)
-            ).wait_recv()
-            if i == 0:
-                chain[...] = rz[0, 0:64].astype(F32)
-            else:
-                chain[...] = chain_step(chain[...], rz[i, 64:192], rz[i, 0:64])
-
-    entering = chain[...].astype(BF16)
-    pmsg[...] = entering
-    p_rows = pl.ds(pl.multiple_of(part * 64, 64), 64)
-    rp[head, p_rows] = entering
-
-    def p_copy(o):
-        return remote(
-            pmsg,
-            rp.at[head, p_rows],
-            p_send.at[o],
-            p_recv.at[x],
-            (z * LANES_X + at_x(o), ten),
-        )
-
-    for o in (2, 1, 3):
-        p_copy(o).start()
     for i in range(LANES_X - 1):
 
         @pl.when(i < x)
@@ -423,7 +463,53 @@
             remote(
                 rx.at[i, 1 - head], rx.at[i, 1 - head], c_send.at[0], c_recv.at[i], (seq, ten)
             ).wait_recv()
-
+            for h in range(2):
+                trans = rx[i, h, 64:192]
+                write = jnp.concatenate([rx[i, h, 0:64], rx[i, h, 192:256]], 0)
+                if i == 0:
+                    before_t[h] = trans.astype(F32)
+                    before_w[h] = write.astype(F32)
+                else:
+                    high, low = split(before_t[h])
+                    both = dot(trans, jnp.concatenate([high, low], 1))
+                    before_t[h] = both[:, :128] + both[:, 128:]
+                    before_w[h] = chain_step(before_w[h], trans, write)
+
+    def z_wait(i):
+        block = rz.at[i, pl.ds(0, 64 if i == 0 else 192)]
+        remote(block, block, z_send.at[0], z_recv.at[i], (seq, ten)).wait_recv()
+
+    for i in range(nz - 2, 0, -1):
+
+        @pl.when(i < z)
+        def _():
+            z_wait(i)
+            chain[...] += apply(rz[i, 0:64], since[...])
+            since[...] = extend(since[...], rz[i, 64:192])
+
+    if nz > 1:
+
+        @pl.when(z > 0)
+        def _():
+            z_wait(0)
+            chain[...] += apply(rz[0, 0:64], since[...])
+
+    entering = chain[...].astype(BF16)
+    pmsg[...] = entering
+    p_rows = pl.ds(pl.multiple_of(part * 64, 64), 64)
+    rp[head, p_rows] = entering
+
+    def p_copy(o):
+        return remote(
+            pmsg,
+            rp.at[head, p_rows],
+            p_send.at[o],
+            p_recv.at[x],
+            (z * LANES_X + at_x(o), ten),
+        )
+
+    for o in (2, 1, 3):
+        p_copy(o).start()
     for o in (1, 3, 2):
         source = at_x(o)
         rows = pl.ds(pl.multiple_of(lax.rem(source, 2) * 64, 64), 64)
@@ -435,13 +521,7 @@
             (seq, ten),
         ).wait_recv()
 
-    state = [rp[h].astype(F32) for h in range(2)]
-    for i in range(LANES_X - 1):
-        for h in range(2):
-            write = jnp.concatenate([rx[i, h, 0:64], rx[i, h, 192:256]], 0)
-            moved = chain_step(state[h], rx[i, h, 64:192], write)
-            state[h] = jnp.where(i < x, moved, state[h])
-
+    state = [apply(rp[h], before_t[h]) + before_w[h] for h in range(2)]
     gain = og_ref[...]
     pieces = []
     for h in range(2):
@@ -476,19 +556,19 @@
     def ring(i, d, p):
         origin = 0 if d <= 2 else 2
         block = xg.at[at_y(ny - ways[i] * origin) * 2 + core, halves[p]]
-        return remote(block, block, g_send.at[i, d, p], g_recv.at[i, d, p], across(i, d))
+        return remote(block, block, g_send.at[i, d - 1, p], g_recv.at[i, d - 1, p], across(i, d))
 
     def got(i, d, p):
         block = xg.at[at_y(ny - ways[i] * d) * 2 + core, halves[p]]
-        remote(block, block, g_send.at[i, d, p], g_recv.at[i, d, p], (seq, ten)).wait_recv()
+        remote(block, block, g_send.at[i, d - 1, p], g_recv.at[i, d - 1, p], (seq, ten)).wait_recv()
 
     def pass_on(i, d, p):
         block = xg.at[at_y(ny - ways[i] * d) * 2 + core, halves[p]]
-        return remote(block, block, f_send.at[i, d, p], f_recv.at[i, d, p], (seq, partner))
+        return remote(block, block, f_send.at[i, d - 1, p], f_recv.at[i, d - 1, p], (seq, partner))
 
     def passed(i, d, p):
         block = xg.at[at_y(ny - ways[i] * d) * 2 + 1 - core, halves[p]]
-        remote(block, block, f_send.at[i, d, p], f_recv.at[i, d, p], (seq, ten)).wait_recv()
+        remote(block, block, f_send.at[i, d - 1, p], f_recv.at[i, d - 1, p], (seq, ten)).wait_recv()
 
     def own_copy():
         return remote(xg.at[ten], xg.at[ten], o_sem.at[0], o_sem.at[1], (seq, partner))
@@ -601,14 +681,14 @@
         return remote(
             psum.at[i, d, halves[p]],
             rs.at[i, d, halves[p]],
-            r_send.at[i, d, p],
-            r_recv.at[i, d, p],
+            r_send.at[i, d - 1, p],
+            r_recv.at[i, d - 1, p],
             across(i, d),
         )
 
     def m_got(i, d, p):
         block = rs.at[i, d, halves[p]]
-        remote(block, block, r_send.at[i, d, p], r_recv.at[i, d, p], (seq, ten)).wait_recv()
+        remote(block, block, r_send.at[i, d - 1, p], r_recv.at[i, d - 1, p], (seq, ten)).wait_recv()
         return rs[i, d, halves[p]].astype(F32)
 
     rows_dev = xg.shape[1] // 2
@@ -653,7 +733,7 @@
         out_ref[halves[p], :] = value.astype(BF16)
 
     for o in range(1, LANES_X):
-        a_copy(o).wait_send()
+        on_first(lambda only_write: a_copy(o, only_write).wait_send())
         p_copy(o).wait_send()
 
         @pl.when(x + o < LANES_X)
@@ -665,7 +745,7 @@
 
         @pl.when(z + o < nz)
         def _():
-            z_copy(o).wait_send()
+            on_first_group(lambda only_write: z_copy(o, only_write).wait_send())
 
     own_copy().wait_send()
     for off in range(1 - reach, reach + 1):
@@ -726,6 +806,9 @@
                 pltpu.VMEM((192, 128), BF16),
                 pltpu.VMEM((nz, 192, 128), BF16),
                 pltpu.VMEM((64, 128), F32),
+                pltpu.VMEM((128, 128), F32),
+                pltpu.VMEM((2, 128, 128), F32),
+                pltpu.VMEM((2, 128, 128), F32),
                 pltpu.VMEM((64, 128), BF16),
                 pltpu.VMEM((2, 128, 128), BF16),
                 pltpu.VMEM((nten, tok, 256), BF16),
@@ -746,15 +829,15 @@
                 dma((nz,)),
                 dma((LANES_X,)),
                 dma((LANES_X,)),
-                dma((2, ny // 2 + 1, 2)),
-                dma((2, ny // 2 + 1, 2)),
-                dma((2, ny // 2 + 1, 2)),
-                dma((2, ny // 2 + 1, 2)),
+                dma((2, ny // 2, 2)),
+                dma((2, ny // 2, 2)),
+                dma((2, ny // 2, 2)),
+                dma((2, ny // 2, 2)),
                 dma((2,)),
                 dma((ny,)),
                 dma((ny,)),
-                dma((2, ny // 2 + 1, 2)),
-                dma((2, ny // 2 + 1, 2)),
+                dma((2, ny // 2, 2)),
+                dma((2, ny // 2, 2)),
             ],
             compiler_params=pltpu.CompilerParams(
                 collective_id=0, has_side_effects=True, vmem_limit_bytes=VMEM_LIMIT

time: 52.4 us -> 51.3 us (0.979)
  the two profiles are of different devices: /device:TPU:384 before, /device:TPU:1 now
where the time goes in v5:
time: 51.3 us; the launch traced here: 51.2 us
  Pallas kernels  50.6 us (99%)
  local copies, waits for them, and re-layouts  0.63 us (1%)
    pallas_call x1, Pallas kernels, per_device(): pl.pallas_call(functools.partial(main_kernel, nz, ny), out_shape=jax.Shap...  50.6 us

profile of v5, /device:TPU:1, one launch (start us, length us, event | category | flops | bytes accessed | tf_op | source)
XLA Modules:
  0.0 51.2 jit_solution(3887404398147900735)
XLA Ops:
  0.0 50.6 %layer.1 = bf16[128,256]{1,0:T(8,128)(2,1)S(1)} custom-call(bf16[256,128]{1,0:T(8,128)(2,1)} %bitcast.7, bf16[512,128]{1,0:T(8,128)(2,1)} %bitcast.5, bf16[512,128]{1,0:T(8,128)(2,1)} %bitcast.6, f32[2,2,128]{2,1,0:T(2,128)} %beta_in.1, f32[2,128]{1,0:T(2,128)} %decay_in.1, s32[4,16]{1,0:T(4,128)} %up_in.1, s32[4,16]{1,0:T(4,128)} %down_in.1, ...), custom_call_target="tpu_custom_call" | custom-call | tf_op jit(solution)/shard_map/layer/pallas_call | solution.py:782
  50.6 0.6 %copy.14 = bf16[128,256]{1,0:T(8,128)(2,1)} copy(bf16[128,256]{1,0:T(8,128)(2,1)S(1)} %layer.1) | data formatting | bytes 131072

commit v6 on v5

--- a/solution.py
+++ b/solution.py
@@ -448,6 +448,42 @@
             for one in b_copies(o):
                 one.start()
 
+    def z_wait(i):
+        block = rz.at[i, pl.ds(0, 64 if i == 0 else 192)]
+        remote(block, block, z_send.at[0], z_recv.at[i], (seq, ten)).wait_recv()
+
+    for i in range(nz - 2, 0, -1):
+
+        @pl.when(i < z)
+        def _():
+            z_wait(i)
+            chain[...] += apply(rz[i, 0:64], since[...])
+            since[...] = extend(since[...], rz[i, 64:192])
+
+    if nz > 1:
+
+        @pl.when(z > 0)
+        def _():
+            z_wait(0)
+            chain[...] += apply(rz[0, 0:64], since[...])
+
+    entering = chain[...].astype(BF16)
+    pmsg[...] = entering
+    p_rows = pl.ds(pl.multiple_of(part * 64, 64), 64)
+    rp[head, p_rows] = entering
+
+    def p_copy(o):
+        return remote(
+            pmsg,
+            rp.at[head, p_rows],
+            p_send.at[o],
+            p_recv.at[x],
+            (z * LANES_X + at_x(o), ten),
+        )
+
+    for o in (2, 1, 3):
+        p_copy(o).start()
+
     for i in range(LANES_X - 1):
 
         @pl.when(i < x)
@@ -475,41 +511,6 @@
                     before_t[h] = both[:, :128] + both[:, 128:]
                     before_w[h] = chain_step(before_w[h], trans, write)
 
-    def z_wait(i):
-        block = rz.at[i, pl.ds(0, 64 if i == 0 else 192)]
-        remote(block, block, z_send.at[0], z_recv.at[i], (seq, ten)).wait_recv()
-
-    for i in range(nz - 2, 0, -1):
-
-        @pl.when(i < z)
-        def _():
-            z_wait(i)
-            chain[...] += apply(rz[i, 0:64], since[...])
-            since[...] = extend(since[...], rz[i, 64:192])
-
-    if nz > 1:
-
-        @pl.when(z > 0)
-        def _():
-            z_wait(0)
-            chain[...] += apply(rz[0, 0:64], since[...])
-
-    entering = chain[...].astype(BF16)
-    pmsg[...] = entering
-    p_rows = pl.ds(pl.multiple_of(part * 64, 64), 64)
-    rp[head, p_rows] = entering
-
-    def p_copy(o):
-        return remote(
-            pmsg,
-            rp.at[head, p_rows],
-            p_send.at[o],
-            p_recv.at[x],
-            (z * LANES_X + at_x(o), ten),
-        )
-
-    for o in (2, 1, 3):
-        p_copy(o).start()
     for o in (1, 3, 2):
         source = at_x(o)
         rows = pl.ds(pl.multiple_of(lax.rem(source, 2) * 64, 64), 64)

time: 51.3 us -> 51.1 us (level)
  the two profiles are of different devices: /device:TPU:1 before, /device:TPU:448 now
where the time goes in v6:
time: 51.1 us; the launch traced here: 51 us
  Pallas kernels  50.3 us (98%)
  local copies, waits for them, and re-layouts  0.63 us (1%)
    pallas_call x1, Pallas kernels, per_device(): pl.pallas_call(functools.partial(main_kernel, nz, ny), out_shape=jax.Shap...  50.3 us

profile of v6, /device:TPU:448, one launch (start us, length us, event | category | flops | bytes accessed | tf_op | source)
XLA Modules:
  0.0 51.0 jit_solution(16990492313817288899)
XLA Ops:
  0.0 50.3 %layer.1 = bf16[128,256]{1,0:T(8,128)(2,1)S(1)} custom-call(bf16[256,128]{1,0:T(8,128)(2,1)} %bitcast.7, bf16[512,128]{1,0:T(8,128)(2,1)} %bitcast.5, bf16[512,128]{1,0:T(8,128)(2,1)} %bitcast.6, f32[2,2,128]{2,1,0:T(2,128)} %beta_in.1, f32[2,128]{1,0:T(2,128)} %decay_in.1, s32[4,16]{1,0:T(4,128)} %up_in.1, s32[4,16]{1,0:T(4,128)} %down_in.1, ...), custom_call_target="tpu_custom_call" | custom-call | tf_op jit(solution)/shard_map/layer/pallas_call | solution.py:783
  50.4 0.6 %copy.14 = bf16[128,256]{1,0:T(8,128)(2,1)} copy(bf16[128,256]{1,0:T(8,128)(2,1)S(1)} %layer.1) | data formatting | bytes 131072

commit v7 on v6

--- a/solution.py
+++ b/solution.py
@@ -277,9 +277,6 @@
     peers += [(lax.rem(z + o, nz) * LANES_X + x, ten) for o in range(1, nz)]
     peers += [(seq, at_y(o) * 2 + core) for o in (1, 2, ny - 2, ny - 1)]
     peers += [(seq, partner)]
-    for peer in peers:
-        pl.semaphore_signal(barrier, inc=1, device_id=peer, device_id_type=MESH)
-
     inputs = (
         (k_in, k_ref),
         (v_in, v_ref),
@@ -297,6 +294,8 @@
     ]
     for load in loads:
         load.start()
+    for peer in peers:
+        pl.semaphore_signal(barrier, inc=1, device_id=peer, device_id_type=MESH)
     load_up = pltpu.make_async_copy(up_hbm, up_v.at[:, pl.ds(0, kept)], wsem.at[0])
     load_down = pltpu.make_async_copy(down_hbm, down_v.at[:, pl.ds(0, kept)], wsem.at[1])
     load_up.start()
@@ -435,7 +434,7 @@
         def _():
             act_on(False)
 
-    for o in range(1, nz):
+    for o in sorted(range(1, nz), key=lambda o: -min(o, nz - o)):
 
         @pl.when(z + o < nz)
         def _():
@@ -554,30 +553,52 @@
     def across(i, d):
         return (seq, at_y(ny + ways[i] * hop[d]) * 2 + core)
 
-    def ring(i, d, p):
-        origin = 0 if d <= 2 else 2
-        block = xg.at[at_y(ny - ways[i] * origin) * 2 + core, halves[p]]
-        return remote(block, block, g_send.at[i, d - 1, p], g_recv.at[i, d - 1, p], across(i, d))
-
-    def got(i, d, p):
-        block = xg.at[at_y(ny - ways[i] * d) * 2 + core, halves[p]]
-        remote(block, block, g_send.at[i, d - 1, p], g_recv.at[i, d - 1, p], (seq, ten)).wait_recv()
-
-    def pass_on(i, d, p):
-        block = xg.at[at_y(ny - ways[i] * d) * 2 + core, halves[p]]
-        return remote(block, block, f_send.at[i, d - 1, p], f_recv.at[i, d - 1, p], (seq, partner))
-
-    def passed(i, d, p):
-        block = xg.at[at_y(ny - ways[i] * d) * 2 + 1 - core, halves[p]]
-        remote(block, block, f_send.at[i, d - 1, p], f_recv.at[i, d - 1, p], (seq, ten)).wait_recv()
+    rows_all = xg.shape[1]
+    quarter = rows_all // 4
+    quarters = [(i, q) for q in range(4) for i in range(2)]
+    crossing = [(i, 2, q * quarter, quarter) for i, q in quarters]
+    crossing += [(i, 1, 0, rows_all) for i in range(2)]
+    crossing += [(i, 3, q * quarter, quarter) for i, q in quarters]
+    crossing += [(i, 4, q * quarter, quarter) for i, q in quarters if q % 2 == i]
+    inside = [(i, d, 0, rows_all) for d in (1, 2) for i in range(2)]
+    inside += [(i, 3, s * 2 * quarter, 2 * quarter) for s in range(2) for i in range(2)]
+    inside += [key for key in crossing if key[1] == 4]
+
+    def block_of(i, d, side, start, count):
+        slot = at_y(ny - ways[i] * d) * 2 + (core if side == 0 else 1 - core)
+        return xg.at[slot, pl.ds(start, count)]
+
+    def ring(key):
+        i, d, start, count = key
+        n = crossing.index(key)
+        block = block_of(i, 0 if d <= 2 else 2, 0, start, count)
+        return remote(block, block, g_send.at[n], g_recv.at[n], across(i, d))
+
+    def got(key):
+        i, d, start, count = key
+        n = crossing.index(key)
+        block = block_of(i, d, 0, start, count)
+        remote(block, block, g_send.at[n], g_recv.at[n], (seq, ten)).wait_recv()
+
+    def pass_on(key):
+        i, d, start, count = key
+        n = inside.index(key)
+        block = block_of(i, d, 0, start, count)
+        return remote(block, block, f_send.at[n], f_recv.at[n], (seq, partner))
+
+    def passed(key):
+        i, d, start, count = key
+        n = inside.index(key)
+        block = block_of(i, d, 1, start, count)
+        remote(block, block, f_send.at[n], f_recv.at[n], (seq, ten)).wait_recv()
 
     def own_copy():
         return remote(xg.at[ten], xg.at[ten], o_sem.at[0], o_sem.at[1], (seq, partner))
 
     for level in (2, 1):
-        for i, d, p in messages:
-            if d == level:
-                ring(i, d, p).start()
+        for key in crossing:
+            if key[1] == level:
+                ring(key).start()
     own_copy().start()
 
     load_up.wait()
@@ -611,38 +632,44 @@
     remote(xg.at[partner], xg.at[partner], o_sem.at[0], o_sem.at[1], (seq, ten)).wait_recv()
     power = absorb(partner, False, power)
 
-    def take(d):
-        for i, e, p in messages:
-            if e == d:
-                got(i, d, p)
-                if d == 2:
-                    for later in (4, 3):
-                        if sent(i, later, p):
-                            ring(i, later, p).start()
-                pass_on(i, d, p).start()
-
     def near(d, power):
         for where in blocks(d):
             power = absorb(where * 2 + core, False, power)
         return power
 
     def far_side(d, power):
-        for i, e, p in messages:
-            if e == d:
-                passed(i, e, p)
+        for key in inside:
+            if key[1] == d:
+                passed(key)
         for where in blocks(d):
             power = absorb(where * 2 + 1 - core, False, power)
         return power
 
-    take(2)
+    for i, q in quarters:
+        start = q * quarter
+        got((i, 2, start, quarter))
+        if q % 2 == i:
+            ring((i, 4, start, quarter)).start()
+        ring((i, 3, start, quarter)).start()
+    for i in range(2):
+        pass_on((i, 2, 0, rows_all)).start()
+    for i in range(2):
+        got((i, 1, 0, rows_all))
+        pass_on((i, 1, 0, rows_all)).start()
     power = near(2, power)
-    take(1)
     power = near(1, power)
     power = far_side(2, power)
     power = far_side(1, power)
-    take(3)
+    for q in range(4):
+        start = q * quarter
+        for i in range(2):
+            got((i, 3, start, quarter))
+            if q % 2 == 1:
+                pass_on((i, 3, start - quarter, 2 * quarter)).start()
+        last = (q % 2, 4, start, quarter)
+        got(last)
+        pass_on(last).start()
     power = near(3, power)
-    take(4)
     power = near(4, power)
     power = far_side(3, power)
     power = far_side(4, power)
@@ -752,9 +779,11 @@
     for off in range(1 - reach, reach + 1):
         s_copy(off).wait_send()
     for i, d, p in messages:
-        ring(i, d, p).wait_send()
-        pass_on(i, d, p).wait_send()
         m_copy(i, d, p).wait_send()
+    for key in crossing:
+        ring(key).wait_send()
+    for key in inside:
+        pass_on(key).wait_send()
 
 
 def solution(mesh):
@@ -830,10 +859,10 @@
                 dma((nz,)),
                 dma((LANES_X,)),
                 dma((LANES_X,)),
-                dma((2, ny // 2, 2)),
-                dma((2, ny // 2, 2)),
-                dma((2, ny // 2, 2)),
-                dma((2, ny // 2, 2)),
+                dma((22,)),
+                dma((22,)),
+                dma((12,)),
+                dma((12,)),
                 dma((2,)),
                 dma((ny,)),
                 dma((ny,)),

time: 51.1 us -> 50.7 us (level)
  the two profiles are of different devices: /device:TPU:448 before, /device:TPU:192 now
where the time goes in v7:
time: 50.7 us; the launch traced here: 50.6 us
  Pallas kernels  49.9 us (98%)
  local copies, waits for them, and re-layouts  0.63 us (1%)
    pallas_call x1, Pallas kernels, per_device(): pl.pallas_call(functools.partial(main_kernel, nz, ny), out_shape=jax.Shap...  49.9 us

profile of v7, /device:TPU:192, one launch (start us, length us, event | category | flops | bytes accessed | tf_op | source)
XLA Modules:
  0.0 50.6 jit_solution(13202305816237937106)
XLA Ops:
  0.0 49.9 %layer.1 = bf16[128,256]{1,0:T(8,128)(2,1)S(1)} custom-call(bf16[256,128]{1,0:T(8,128)(2,1)} %bitcast.7, bf16[512,128]{1,0:T(8,128)(2,1)} %bitcast.5, bf16[512,128]{1,0:T(8,128)(2,1)} %bitcast.6, f32[2,2,128]{2,1,0:T(2,128)} %beta_in.1, f32[2,128]{1,0:T(2,128)} %decay_in.1, s32[4,16]{1,0:T(4,128)} %up_in.1, s32[4,16]{1,0:T(4,128)} %down_in.1, ...), custom_call_target="tpu_custom_call" | custom-call | tf_op jit(solution)/shard_map/layer/pallas_call | solution.py:812
  49.9 0.6 %copy.14 = bf16[128,256]{1,0:T(8,128)(2,1)} copy(bf16[128,256]{1,0:T(8,128)(2,1)S(1)} %layer.1) | data formatting | bytes 131072

commit v8 on v7

--- a/solution.py
+++ b/solution.py
@@ -232,6 +232,7 @@
     rp,
     xg,
     acc,
+    row_power,
     act,
     pair_out,
     pair_in,
@@ -605,9 +606,9 @@
     load_down.wait()
     load_table.wait()
 
-    def absorb(slot, first, power):
+    def absorb(slot, first=False):
         wide = xg[slot].astype(F32)
-        power = power + jnp.sum(wide * wide, -1, keepdims=True)
+        squares = jnp.sum(wide * wide, -1, keepdims=True)
         scaled = (wide * fg_ref[slot]).astype(BF16)
         weights = jnp.concatenate(
             [
@@ -621,61 +622,83 @@
         term = dot(scaled, weights)
         if first:
             acc[...] = term
+            row_power[...] = squares
         else:
             acc[...] += term
-        return power
-
-    def blocks(d):
-        return [at_y(d)] if d == reach else [at_y(ny - d), at_y(d)]
-
-    power = absorb(ten, True, jnp.zeros((xg.shape[1], 1), F32))
+            row_power[...] += squares
+
+    sources = [(0, 2), (1, 2), (0, 1), (1, 1), (0, 3), (1, 3), (0, 4)]
+
+    def source_y(source):
+        return at_y(ny - ways[source[0]] * source[1])
+
+    def keys_of(table, source):
+        i, d = source
+        return [key for key in table if key[1] == d and (d == 4 or key[0] == i)]
+
+    def handle(source):
+        d = source[1]
+        for key in keys_of(crossing, source):
+            i, _, start, count = key
+            got(key)
+            if d == 2:
+                if (start // quarter) % 2 == i:
+                    ring((i, 4, start, count)).start()
+                ring((i, 3, start, count)).start()
+            elif d == 3 and (start // quarter) % 2 == 1:
+                pass_on((i, 3, start - quarter, 2 * quarter)).start()
+            elif d == 4:
+                pass_on(key).start()
+        if d <= 2:
+            pass_on(keys_of(inside, source)[0]).start()
+
+    def finish(source):
+        for key in keys_of(inside, source):
+            passed(key)
+
+    def early(source, act_on):
+        @pl.when(source_y(source) != 0)
+        def _():
+            act_on(source)
+
+    def late(source, act_on):
+        @pl.when(source_y(source) == 0)
+        def _():
+            act_on(source)
+
+    def near(source):
+        absorb(source_y(source) * 2 + core)
+
+    def far(source):
+        finish(source)
+        absorb(source_y(source) * 2 + 1 - core)
+
+    absorb(ten, True)
+    for group in (sources[:4], sources[4:]):
+        for source in group:
+            early(source, handle)
+        for source in group:
+            early(source, near)
+        for source in group:
+            early(source, far)
     remote(xg.at[partner], xg.at[partner], o_sem.at[0], o_sem.at[1], (seq, ten)).wait_recv()
-    power = absorb(partner, False, power)
-
-    def near(d, power):
-        for where in blocks(d):
-            power = absorb(where * 2 + core, False, power)
-        return power
-
-    def far_side(d, power):
-        for key in inside:
-            if key[1] == d:
-                passed(key)
-        for where in blocks(d):
-            power = absorb(where * 2 + 1 - core, False, power)
-        return power
-
-    for i, q in quarters:
-        start = q * quarter
-        got((i, 2, start, quarter))
-        if q % 2 == i:
-            ring((i, 4, start, quarter)).start()
-        ring((i, 3, start, quarter)).start()
-    for i in range(2):
-        pass_on((i, 2, 0, rows_all)).start()
-    for i in range(2):
-        got((i, 1, 0, rows_all))
-        pass_on((i, 1, 0, rows_all)).start()
-    power = near(2, power)
-    power = near(1, power)
-    power = far_side(2, power)
-    power = far_side(1, power)
-    for q in range(4):
-        start = q * quarter
-        for i in range(2):
-            got((i, 3, start, quarter))
-            if q % 2 == 1:
-                pass_on((i, 3, start - quarter, 2 * quarter)).start()
-        last = (q % 2, 4, start, quarter)
-        got(last)
-        pass_on(last).start()
-    power = near(3, power)
-    power = near(4, power)
-    power = far_side(3, power)
-    power = far_side(4, power)
+    absorb(partner)
+    for source in sources:
+        late(source, handle)
+
+    @pl.when(y != 0)
+    def _():
+        absorb(core)
+
+    for source in sources:
+        late(source, finish)
+
+    @pl.when(y != 0)
+    def _():
+        absorb(1 - core)
 
     width = 256 * xg.shape[0]
-    scale = lax.rsqrt(power / width + 1e-05)
+    scale = lax.rsqrt(row_power[...] / width + 1e-05)
     act[...] = jax.nn.gelu(acc[...] * scale).astype(BF16)
 
     def share(slot):
@@ -843,6 +866,7 @@
                 pltpu.VMEM((2, 128, 128), BF16),
                 pltpu.VMEM((nten, tok, 256), BF16),
                 pltpu.VMEM((tok, groups * 128), F32),
+                pltpu.VMEM((tok, 1), F32),
                 pltpu.VMEM((tok, groups * 128), BF16),
                 pltpu.VMEM((ny, tok, 256), BF16),
                 pltpu.VMEM((ny, tok, 256), BF16),

time: 50.7 us -> 56.5 us (1.11)
  Pallas kernels: 49.9 us -> 55.8 us
    pallas_call x1, Pallas kernels: 49.9 us -> 55.8 us  [per_device(): pl.pallas_call(functools.partial(main_kernel, nz, ny), out_shape=jax.Shap...]
where the time goes in v8:
time: 56.5 us; the launch traced here: 56.4 us
  Pallas kernels  55.8 us (99%)
  local copies, waits for them, and re-layouts  0.63 us (1%)
    pallas_call x1, Pallas kernels, per_device(): pl.pallas_call(functools.partial(main_kernel, nz, ny), out_shape=jax.Shap...  55.8 us

profile of v8, /device:TPU:192, one launch (start us, length us, event | category | flops | bytes accessed | tf_op | source)
XLA Modules:
  0.0 56.4 jit_solution(3087658368941652714)
XLA Ops:
  0.0 55.8 %layer.1 = bf16[128,256]{1,0:T(8,128)(2,1)S(1)} custom-call(bf16[256,128]{1,0:T(8,128)(2,1)} %bitcast.7, bf16[512,128]{1,0:T(8,128)(2,1)} %bitcast.5, bf16[512,128]{1,0:T(8,128)(2,1)} %bitcast.6, f32[2,2,128]{2,1,0:T(2,128)} %beta_in.1, f32[2,128]{1,0:T(2,128)} %decay_in.1, s32[4,16]{1,0:T(4,128)} %up_in.1, s32[4,16]{1,0:T(4,128)} %down_in.1, ...), custom_call_target="tpu_custom_call" | custom-call | tf_op jit(solution)/shard_map/layer/pallas_call | solution.py:835
  55.8 0.6 %copy.14 = bf16[128,256]{1,0:T(8,128)(2,1)} copy(bf16[128,256]{1,0:T(8,128)(2,1)S(1)} %layer.1) | data formatting | bytes 131072

commit v9 on v8

--- a/solution.py
+++ b/solution.py
@@ -674,17 +674,19 @@
         absorb(source_y(source) * 2 + 1 - core)
 
     absorb(ten, True)
-    for group in (sources[:4], sources[4:]):
-        for source in group:
-            early(source, handle)
-        for source in group:
-            early(source, near)
-        for source in group:
-            early(source, far)
+    for act_on in (handle, near, far):
+        for source in sources[:4]:
+            early(source, act_on)
+    for source in sources[:4]:
+        late(source, handle)
     remote(xg.at[partner], xg.at[partner], o_sem.at[0], o_sem.at[1], (seq, ten)).wait_recv()
     absorb(partner)
-    for source in sources:
-        late(source, handle)
+    for when in (early, late):
+        for source in sources[4:]:
+            when(source, handle)
+    for act_on in (near, far):
+        for source in sources[4:]:
+            early(source, act_on)
 
     @pl.when(y != 0)
     def _():

time: 56.5 us -> 53.6 us (0.949)
  the two profiles are of different devices: /device:TPU:192 before, /device:TPU:264 now
where the time goes in v9:
time: 53.6 us; the launch traced here: 53.4 us
  Pallas kernels  52.8 us (99%)
  local copies, waits for them, and re-layouts  0.63 us (1%)
    pallas_call x1, Pallas kernels, per_device(): pl.pallas_call(functools.partial(main_kernel, nz, ny), out_shape=jax.Shap...  52.8 us

profile of v9, /device:TPU:264, one launch (start us, length us, event | category | flops | bytes accessed | tf_op | source)
XLA Modules:
  0.0 53.4 jit_solution(11725081911825334905)
XLA Ops:
  0.0 52.8 %layer.1 = bf16[128,256]{1,0:T(8,128)(2,1)S(1)} custom-call(bf16[256,128]{1,0:T(8,128)(2,1)} %bitcast.7, bf16[512,128]{1,0:T(8,128)(2,1)} %bitcast.5, bf16[512,128]{1,0:T(8,128)(2,1)} %bitcast.6, f32[2,2,128]{2,1,0:T(2,128)} %beta_in.1, f32[2,128]{1,0:T(2,128)} %decay_in.1, s32[4,16]{1,0:T(4,128)} %up_in.1, s32[4,16]{1,0:T(4,128)} %down_in.1, ...), custom_call_target="tpu_custom_call" | custom-call | tf_op jit(solution)/shard_map/layer/pallas_call | solution.py:837
  52.8 0.6 %copy.14 = bf16[128,256]{1,0:T(8,128)(2,1)} copy(bf16[128,256]{1,0:T(8,128)(2,1)S(1)} %layer.1) | data formatting | bytes 131072

commit v10 on v7

--- a/solution.py
+++ b/solution.py
@@ -146,21 +146,26 @@
             0,
         )
         a_val = a * beta_r
-        a_key = a_val * (jnp.exp(run_r) * rk_row)
         ah, al = split(a_val)
         u = dot(ah, v) + dot(al, v)
-        ah, al = split(a_key)
-        w = dot(ah, k) + dot(al, k)
         last = run_c[span - 1 : span, :]
         remain = jnp.exp(last - run_c) * rk_col
         uh, ul = split(u * remain)
         write_t = dot(uh, k, (0, 0)) + dot(ul, k, (0, 0))
-        wh, wl = split(w * remain)
-        trans = jnp.exp(last) * eye - dot(k, wh, (0, 0)) - dot(k, wl, (0, 0))
         tw_ref[h, 0:64, :] = write_t[:64].astype(BF16)
-        tw_ref[h, 64:192, :] = trans.astype(BF16)
         tw_ref[h, 192:256, :] = write_t[64:].astype(BF16)
-        left.append((k, u, w, rk_row, run_r, tok_col[:, h : h + 1]))
+        mids[h] = (a_val, last, remain, u)
+
+    def transitions():
+        for h in range(heads):
+            k, v, rk_col, rk_row, run_c, run_r, beta_r, low = keep[h]
+            a_val, last, remain, u = mids[h]
+            ah, al = split(a_val * (jnp.exp(run_r) * rk_row))
+            w = dot(ah, k) + dot(al, k)
+            wh, wl = split(w * remain)
+            trans = jnp.exp(last) * eye - dot(k, wh, (0, 0)) - dot(k, wl, (0, 0))
+            tw_ref[h, 64:192, :] = trans.astype(BF16)
+            left.append((k, u, w, rk_row, run_r, tok_col[:, h : h + 1]))
 
     def queries():
         q_all = q_ref[...]
@@ -178,7 +183,7 @@
             qt_ref[h] = (jnp.exp(tok_run) * rq) * q - mixed[:, :128]
             lo_ref[h] = mixed[:, 128:]
 
-    return queries
+    return transitions, queries
 
 
 def chain_step(state, trans, write):
@@ -302,7 +307,7 @@
     load_down.start()
     for load in loads:
         load.wait()
-    queries = local_terms(q_ref, k_ref, v_ref, beta_ref, decay_ref, rx.at[x], qt_ref, lo_ref)
+    transitions, queries = local_terms(q_ref, k_ref, v_ref, beta_ref, decay_ref, rx.at[x], qt_ref, lo_ref)
     pl.semaphore_wait(barrier, len(peers))
 
     def remote(src, dst, send, recv, peer):
@@ -376,8 +381,17 @@
             ),
         )
 
-    for o in (2, 1, 3):
-        on_first(lambda only_write: a_copy(o, only_write).start())
+    @pl.when(seq == 0)
+    def _():
+        for o in (2, 1, 3):
+            a_copy(o, True).start()
+
+    transitions()
+
+    @pl.when(seq != 0)
+    def _():
+        for o in (2, 1, 3):
+            a_copy(o, False).start()
 
     chain[...] = jnp.zeros_like(chain)
     eye = (iota((128, 128), 0) == iota((128, 128), 1)).astype(F32)

time: 50.7 us -> 51.3 us (1.012)
  Pallas kernels: 49.9 us -> 50.5 us
    pallas_call x1, Pallas kernels: 49.9 us -> 50.5 us  [per_device(): pl.pallas_call(functools.partial(main_kernel, nz, ny), out_shape=jax.Shap...]
where the time goes in v10:
time: 51.3 us; the launch traced here: 51.2 us
  Pallas kernels  50.5 us (98%)
  local copies, waits for them, and re-layouts  0.63 us (1%)
    pallas_call x1, Pallas kernels, per_device(): pl.pallas_call(functools.partial(main_kernel, nz, ny), out_shape=jax.Shap...  50.5 us

profile of v10, /device:TPU:192, one launch (start us, length us, event | category | flops | bytes accessed | tf_op | source)
XLA Modules:
  0.0 51.2 jit_solution(18324616128765607120)
XLA Ops:
  0.0 50.5 %layer.1 = bf16[128,256]{1,0:T(8,128)(2,1)S(1)} custom-call(bf16[256,128]{1,0:T(8,128)(2,1)} %bitcast.7, bf16[512,128]{1,0:T(8,128)(2,1)} %bitcast.5, bf16[512,128]{1,0:T(8,128)(2,1)} %bitcast.6, f32[2,2,128]{2,1,0:T(2,128)} %beta_in.1, f32[2,128]{1,0:T(2,128)} %decay_in.1, s32[4,16]{1,0:T(4,128)} %up_in.1, s32[4,16]{1,0:T(4,128)} %down_in.1, ...), custom_call_target="tpu_custom_call" | custom-call | tf_op jit(solution)/shard_map/layer/pallas_call | solution.py:826
  50.5 0.6 %copy.14 = bf16[128,256]{1,0:T(8,128)(2,1)} copy(bf16[128,256]{1,0:T(8,128)(2,1)S(1)} %layer.1) | data formatting | bytes 131072
